TPU v7x, 32 devices: a whole 2x2x4 slice. The times are simulated.
32 devices in a mesh: groups: 2 (over y), tap: 4 (over z), tm: 2 (over x), lag: 2 (over core).
Axes of the slice: x: 2, y: 2, z: 4, core: 2. Of those that a mesh axis runs over, the one named last changes fastest.
Arguments:
- raw_strain: bfloat16 [2048, 1024], P(('groups', 'tap'), 'tm'), parts along dimension 0, may hold values from -4000 to 4000
- spatial_filter: float32 [33], replicated, may hold values from -0.35 to 0.35
- temporal_filter: float32 [255], replicated, may hold values from -0.125 to 0.125
- dest_blocks: int32 [16, 2], P('groups'), parts along dimension 0, may hold values from 0 to 7, as said below
- partner_codes: int32 [16, 128, 64], P(('groups', 'tap', 'lag'), 'tm'), parts along dimension 0, may hold values from 0 to 255, as said below
Outputs:
- coherence: bfloat16 [16, 128, 64, 512], P(('groups', 'tap', 'lag'), 'tm'), parts along dimension 0
There are 2 independent parts, one for each index of `groups`. A program takes and returns all parts, laid end to end along the dimension named above; an argument that names none is the same for every part. Nothing has to cross between parts.
Inputs may be any that keep to these rules, and one draw needn't show every extreme that they name: With n the number of devices along lag, the values dest_blocks[s, j] // n of one row s are distinct and all differ from s // n. `partner_codes`: the 64 codes of one source tap are distinct. Within every source block, each destination slot 0 .. 1 is named by the codes of some tap of that block.
All inputs are finite; a program needn't handle non-finite values.
Results may differ from a plain program's by a relative error of at most 0.022.
Values may be sent and summed in bfloat16 or wider, within the bound.
No kernel may reach another device: no remote copies, remote signals or barrier semaphores. Data moves between devices by JAX's collectives and lax.ppermute only.
A program may use at most 128 MiB of HBM per device.

v0:
```python
import math

import jax
import jax.numpy as jnp
from jax import lax
from jax.sharding import PartitionSpec as P

LAG_COUNT = 512


EPSILON = 1e-06


def extended(cells, sides, width):
    for axis, dim in sides:
        count = lax.axis_size(axis)
        ends = count - 1
        head = lax.slice_in_dim(cells, 0, width, axis=dim)
        tail = lax.slice_in_dim(cells, cells.shape[dim] - width, cells.shape[dim], axis=dim)
        cells = jnp.concatenate(
            [
                lax.ppermute(tail, axis, [(i, (i + 1) % count) for i in range(ends)]),
                cells,
                lax.ppermute(head, axis, [((i + 1) % count, i) for i in range(ends)]),
            ],
            axis=dim,
        )
    return cells


def band_matrix(vector, row_count, col_count):
    length = vector.shape[0]
    padded = jnp.concatenate([vector, jnp.zeros((col_count + 1 - length,), vector.dtype)])
    repeated = jnp.tile(padded, row_count)[: row_count * col_count]
    return repeated.reshape(row_count, col_count)


def split_parts(matrix):
    high_part = matrix.astype(jnp.bfloat16)
    low_part = (matrix - high_part.astype(jnp.float32)).astype(jnp.bfloat16)
    return (high_part, low_part)


def whiten(strain_ext, row_count, spatial_filter, temporal_filter):
    spatial = band_matrix(spatial_filter, row_count, strain_ext.shape[0])
    spatial_high, spatial_low = split_parts(spatial)
    smooth = jnp.einsum("cr,rt->ct", spatial_high, strain_ext, preferred_element_type=jnp.float32)
    smooth = smooth + jnp.einsum(
        "cr,rt->ct", spatial_low, strain_ext, preferred_element_type=jnp.float32
    )
    smooth = smooth.astype(jnp.bfloat16)
    time_half = temporal_filter.shape[0] // 2
    smooth_ext = extended(smooth, (("tm", 1),), time_half)
    temporal = band_matrix(temporal_filter, smooth.shape[1], smooth_ext.shape[1])
    temporal_high, temporal_low = split_parts(temporal)
    whitened = jnp.einsum(
        "cs,ts->ct", smooth_ext, temporal_high, preferred_element_type=jnp.float32
    )
    whitened = whitened + jnp.einsum(
        "cs,ts->ct", smooth_ext, temporal_low, preferred_element_type=jnp.float32
    )
    return whitened.astype(jnp.bfloat16)


def lag_products(buffer, own_row, row_index, lag_count):
    time_total = own_row.shape[0]
    lag_tile = lag_count // 4
    lag_half = lag_count // 2
    picked = jnp.take(buffer, row_index, axis=0)
    padded = jnp.pad(picked, ((0, 0), (lag_half, lag_half)))
    shifted = jnp.concatenate(
        [
            padded[:, shift_step * lag_tile : shift_step * lag_tile + time_total + lag_tile]
            for shift_step in range(4)
        ],
        axis=0,
    )
    toeplitz = band_matrix(own_row, lag_tile, time_total + lag_tile)
    products = lax.dot_general(
        shifted, toeplitz, (((1,), (1,)), ((), ())), preferred_element_type=jnp.float32
    )
    return products.reshape(4, -1, lag_tile).transpose(1, 0, 2).reshape(-1, lag_count)


def per_device(raw_strain, spatial_filter, temporal_filter, dest_blocks, partner_codes):
    taps_here, steps_time = raw_strain.shape
    lag_devices = lax.axis_size("lag")
    tap_devices = lax.axis_size("tap")
    time_devices = lax.axis_size("tm")
    block_taps = taps_here // lag_devices
    lag_index = lax.axis_index("lag")
    tap_index = lax.axis_index("tap")
    spatial_halfwidth = spatial_filter.shape[0] // 2
    strain_ext = extended(raw_strain, (("tap", 0),), spatial_halfwidth)
    whitened = whiten(strain_ext, taps_here, spatial_filter, temporal_filter)
    dest_count = dest_blocks.shape[1]
    by_owner = dest_blocks.reshape(tap_devices, lag_devices, dest_count)
    requests = lax.dynamic_index_in_dim(by_owner, lag_index, 1, keepdims=False)
    req_owner = requests // lag_devices
    req_local = requests % lag_devices
    owner_match = req_owner == tap_index
    local_match = req_local[:, :, None] == jnp.arange(lag_devices, dtype=jnp.int32)[None, None, :]
    selector = jnp.sum(
        jnp.logical_and(owner_match[:, :, None], local_match).astype(jnp.float32), axis=1
    )
    blocks_here = whitened.reshape(lag_devices, block_taps, steps_time)
    outgoing = jnp.einsum(
        "il,lbt->ibt",
        selector.astype(jnp.bfloat16),
        blocks_here,
        preferred_element_type=jnp.float32,
    ).astype(jnp.bfloat16)
    my_blocks = lax.dynamic_index_in_dim(requests, tap_index, 0, keepdims=False)
    my_owners = my_blocks // lag_devices
    code_table = partner_codes[0]
    spread_out = jnp.broadcast_to(
        outgoing[:, None], (tap_devices, time_devices, block_taps, steps_time)
    )
    spread_out = spread_out.reshape(tap_devices * time_devices, block_taps, steps_time)
    arrived = lax.all_to_all(spread_out, ("tap", "tm"), split_axis=0, concat_axis=2, tiled=True)
    arrived = arrived.reshape(block_taps, tap_devices, time_devices * steps_time)
    picked = jnp.take(arrived, my_owners, axis=1)
    buffer = picked.reshape(block_taps * dest_count, -1)
    row_index = code_table % block_taps * dest_count + code_table // block_taps
    own_block = lax.dynamic_slice_in_dim(whitened, lag_index * block_taps, block_taps, 0)
    own_rows = lax.all_to_all(own_block, "tm", split_axis=0, concat_axis=1, tiled=True)
    time_total = own_rows.shape[1]
    energy_own = jnp.sum(jnp.square(own_rows.astype(jnp.float32)), axis=1) / time_total + EPSILON
    energy_buffer = jnp.sum(jnp.square(buffer.astype(jnp.float32)), axis=1) / time_total + EPSILON
    energy_partner = jnp.take(energy_buffer, row_index)
    source_count = own_rows.shape[0]
    partner_count = row_index.shape[1]
    group_size = math.gcd(source_count, 8)
    rows_grouped = own_rows.reshape(source_count // group_size, group_size, time_total)
    index_grouped = row_index.reshape(source_count // group_size, group_size, partner_count)

    def tap_lag_offsets(own_row, indices):
        return lag_products(buffer, own_row, indices, LAG_COUNT)

    def group_products(pieces):
        return jax.vmap(tap_lag_offsets)(pieces[0], pieces[1])

    products = lax.map(group_products, (rows_grouped, index_grouped))
    products = products.reshape(source_count, partner_count, LAG_COUNT)
    norm_scale = jnp.sqrt(energy_own[:, None] * energy_partner) * jnp.sqrt(jnp.float32(time_total))
    coherence = (products / norm_scale[:, :, None]).astype(jnp.bfloat16)
    return coherence[None]


def solution(mesh):
    placed = (
        P(("groups", "tap"), "tm"),
        P(),
        P(),
        P("groups", None),
        P(("groups", "tap", "lag"), "tm", None),
    )
    return jax.shard_map(
        per_device,
        mesh=mesh,
        in_specs=placed,
        out_specs=P(("groups", "tap", "lag"), "tm", None, None),
        check_vma=False,
    )
```

profile of v0, /device:TPU:0, one launch (start us, length us, event | category | flops | bytes accessed | tf_op | source)
XLA Modules:
  0.0 268.1 jit_solution(12425569988358387064)
XLA Ops:
  2.6 6.2 %collective-permute-start = (bf16[16,512]{1,0:T(8,128)(2,1)}, bf16[16,512]{1,0:T(8,128)(2,1)}, u32[]{:S(2)}, u32[]{:S(2)}) collective-permute-start(bf16[16,512]{1,0:T(8,128)(2,1)} %get-tuple-element.88), channel_id=1, source_target_pairs={{0,4},{4,8},{8,12},{1,5},{5,9},{9,13},{2,6},{6,10},{10,14},{3,7},{... | collective-permute-start | bytes 49160 | tf_op jit(solution)/shard_map/ppermute | solution.py:22
  14.4 3.1 %reshape.419 = f32[512,766]{1,0:T(8,128)S(1)} reshape(f32[392192]{0:T(1024)} %slice.64) | data formatting | bytes 3137536 | tf_op jit(solution)/shard_map/reshape | solution.py:35
  19.7 3.9 %collective-permute-start.2 = (bf16[256,127]{1,0:T(8,128)(2,1)S(1)}, bf16[256,127]{1,0:T(8,128)(2,1)S(1)}, u32[]{:S(2)}, u32[]{:S(2)}) collective-permute-start(bf16[256,127]{1,0:T(8,128)(2,1)S(1)} %get-tuple-element.85), channel_id=1, source_target_pairs={{0,2},{1,3},{4,6},{5,7},{8,10},{9,11},{12,14},{13,15},{16,18},{17,... | collective-permute-start | bytes 195080 | tf_op jit(solution)/shard_map/ppermute | solution.py:22
  25.4 4.3 %collective-permute-done.3 = bf16[256,127]{1,0:T(8,128)(2,1)S(1)} collective-permute-done((bf16[256,127]{1,0:T(8,128)(2,1)S(1)}, bf16[256,127]{1,0:T(8,128)(2,1)S(1)}, u32[]{:S(2)}, u32[]{:S(2)}) %collective-permute-start.3) | collective-permute-done | bytes 65056 | tf_op jit(solution)/shard_map/ppermute | solution.py:24
  31.2 3.4 %all-to-all-start.1 = ((bf16[2,64,512]{2,1,0:T(8,128)(2,1)}), bf16[2,64,512]{2,1,0:T(8,128)(2,1)S(1)}, u32[]{:S(2)}, u32[]{:S(2)}) async-start(bf16[2,64,512]{2,1,0:T(8,128)(2,1)} %bitcast.15), calls=%async_computation.1 | async-start | bytes 262144 | tf_op jit(solution)/shard_map/all_to_all | solution.py:126
  35.6 3.5 %all-to-all-done.1 = bf16[2,64,512]{2,1,0:T(8,128)(2,1)S(1)} async-done(((bf16[2,64,512]{2,1,0:T(8,128)(2,1)}), bf16[2,64,512]{2,1,0:T(8,128)(2,1)S(1)}, u32[]{:S(2)}, u32[]{:S(2)}) %all-to-all-start.1) | async-done | bytes 131104 | tf_op jit(solution)/shard_map/all_to_all | solution.py:126
  40.2 3.8 %all-to-all-start = ((bf16[8,128,512]{1,2,0:T(8,128)(2,1)}), bf16[8,128,512]{1,2,0:T(8,128)(2,1)S(1)}, u32[]{:S(2)}, u32[]{:S(2)}) async-start(bf16[8,128,512]{1,2,0:T(8,128)(2,1)} %bitcast.9), calls=%async_computation | async-start | bytes 2097152 | tf_op jit(solution)/shard_map/all_to_all | solution.py:120
  45.0 21.9 %all-to-all-done = bf16[8,128,512]{1,2,0:T(8,128)(2,1)S(1)} async-done(((bf16[8,128,512]{1,2,0:T(8,128)(2,1)}), bf16[8,128,512]{1,2,0:T(8,128)(2,1)S(1)}, u32[]{:S(2)}, u32[]{:S(2)}) %all-to-all-start) | async-done | bytes 1048608 | tf_op jit(solution)/shard_map/all_to_all | solution.py:120
  68.6 25.7 %gather_fusion.2 = f32[4096]{0:T(1024)S(1)} fusion(f32[256]{0:T(256)S(1)} %add.219, s32[4096]{0:T(1024)S(1)} %broadcast_clamp_fusion), kind=kCustom, calls=%fused_computation.2 | custom fusion | bytes 49152 | tf_op jit(solution)/shard_map/jit(_take)/gather | solution.py:130
  95.3 167.5 %while.12 = (s32[]{:T(128)}, f32[8,8,64,512]{3,2,1,0:T(8,128)}, s32[8,8,64]{2,1,0:T(8,128)S(1)}, bf16[256,1024]{1,0:T(8,128)(2,1)S(1)}, bf16[8,8,1024]{2,1,0:T(8,128)(2,1)S(1)}, /*index=5*/s32[]{:T(128)}, bf16[]{:T(256)}) while((s32[]{:T(128)}, f32[8,8,64,512]{3,2,1,0:T(8,128)}, s32[8,8,64]{2,1,0:T(8,128)S(1)}, ...), condition=%wide.region_2.3_spmd, body=%wide.region_1.2_spmd.sunk | while | flops 623384064 | bytes 57009364 | solution.py:143
  95.6 2.1 gather_fusion
  99.1 5.2 %reshape.464 = bf16[1180672]{0:T(1024)(128)(2,1)} reshape(bf16[8,128,1153]{2,1,0:T(8,128)(2,1)S(1)} %tile.36) | data formatting | bytes 4722688 | tf_op jit(solution)/shard_map/while
  104.3 4.2 %tile.37 = bf16[8,147584]{1,0:T(8,128)(2,1)S(1)} reshape(bf16[1180672]{0:T(1024)(128)(2,1)} %reshape.464) | data formatting | bytes 4722688 | tf_op jit(solution)/shard_map/while/body/eval_jaxpr/vmap()/tile | solution.py:34
  116.5 2.1 gather_fusion
  119.9 5.2 %reshape.464 = bf16[1180672]{0:T(1024)(128)(2,1)} reshape(bf16[8,128,1153]{2,1,0:T(8,128)(2,1)S(1)} %tile.36) | data formatting | bytes 4722688 | tf_op jit(solution)/shard_map/while
  125.2 4.2 %tile.37 = bf16[8,147584]{1,0:T(8,128)(2,1)S(1)} reshape(bf16[1180672]{0:T(1024)(128)(2,1)} %reshape.464) | data formatting | bytes 4722688 | tf_op jit(solution)/shard_map/while/body/eval_jaxpr/vmap()/tile | solution.py:34
  137.4 2.1 gather_fusion
  140.9 5.2 %reshape.464 = bf16[1180672]{0:T(1024)(128)(2,1)} reshape(bf16[8,128,1153]{2,1,0:T(8,128)(2,1)S(1)} %tile.36) | data formatting | bytes 4722688 | tf_op jit(solution)/shard_map/while
  146.1 4.2 %tile.37 = bf16[8,147584]{1,0:T(8,128)(2,1)S(1)} reshape(bf16[1180672]{0:T(1024)(128)(2,1)} %reshape.464) | data formatting | bytes 4722688 | tf_op jit(solution)/shard_map/while/body/eval_jaxpr/vmap()/tile | solution.py:34
  158.3 2.1 gather_fusion
  161.8 5.2 %reshape.464 = bf16[1180672]{0:T(1024)(128)(2,1)} reshape(bf16[8,128,1153]{2,1,0:T(8,128)(2,1)S(1)} %tile.36) | data formatting | bytes 4722688 | tf_op jit(solution)/shard_map/while
  167.0 4.2 %tile.37 = bf16[8,147584]{1,0:T(8,128)(2,1)S(1)} reshape(bf16[1180672]{0:T(1024)(128)(2,1)} %reshape.464) | data formatting | bytes 4722688 | tf_op jit(solution)/shard_map/while/body/eval_jaxpr/vmap()/tile | solution.py:34
  179.2 2.1 gather_fusion
  182.7 5.2 %reshape.464 = bf16[1180672]{0:T(1024)(128)(2,1)} reshape(bf16[8,128,1153]{2,1,0:T(8,128)(2,1)S(1)} %tile.36) | data formatting | bytes 4722688 | tf_op jit(solution)/shard_map/while
  187.9 4.2 %tile.37 = bf16[8,147584]{1,0:T(8,128)(2,1)S(1)} reshape(bf16[1180672]{0:T(1024)(128)(2,1)} %reshape.464) | data formatting | bytes 4722688 | tf_op jit(solution)/shard_map/while/body/eval_jaxpr/vmap()/tile | solution.py:34
  203.6 5.2 %reshape.464 = bf16[1180672]{0:T(1024)(128)(2,1)} reshape(bf16[8,128,1153]{2,1,0:T(8,128)(2,1)S(1)} %tile.36) | data formatting | bytes 4722688 | tf_op jit(solution)/shard_map/while
  208.8 4.2 %tile.37 = bf16[8,147584]{1,0:T(8,128)(2,1)S(1)} reshape(bf16[1180672]{0:T(1024)(128)(2,1)} %reshape.464) | data formatting | bytes 4722688 | tf_op jit(solution)/shard_map/while/body/eval_jaxpr/vmap()/tile | solution.py:34
  224.5 5.2 %reshape.464 = bf16[1180672]{0:T(1024)(128)(2,1)} reshape(bf16[8,128,1153]{2,1,0:T(8,128)(2,1)S(1)} %tile.36) | data formatting | bytes 4722688 | tf_op jit(solution)/shard_map/while
  229.7 4.2 %tile.37 = bf16[8,147584]{1,0:T(8,128)(2,1)S(1)} reshape(bf16[1180672]{0:T(1024)(128)(2,1)} %reshape.464) | data formatting | bytes 4722688 | tf_op jit(solution)/shard_map/while/body/eval_jaxpr/vmap()/tile | solution.py:34
  245.4 5.2 %reshape.464 = bf16[1180672]{0:T(1024)(128)(2,1)} reshape(bf16[8,128,1153]{2,1,0:T(8,128)(2,1)S(1)} %tile.36) | data formatting | bytes 4722688 | tf_op jit(solution)/shard_map/while
  250.7 4.2 %tile.37 = bf16[8,147584]{1,0:T(8,128)(2,1)S(1)} reshape(bf16[1180672]{0:T(1024)(128)(2,1)} %reshape.464) | data formatting | bytes 4722688 | tf_op jit(solution)/shard_map/while/body/eval_jaxpr/vmap()/tile | solution.py:34
  262.9 5.2 %fusion.11 = bf16[1,64,64,512]{3,2,1,0:T(8,128)(2,1)} fusion(f32[64,64]{1,0:T(8,128)S(1)} %sqrt_multiply_fusion, f32[1,64,64,512]{3,2,1,0:T(8,128)} %bitcast.135), kind=kLoop, calls=%fused_computation.26 | loop fusion | flops 4194304 | bytes 12599296 | tf_op jit(solution)/shard_map/convert_element_type | solution.py:146
  (217 shorter events, 100.2 us)
Async XLA Ops:
  1.3 16.9 %collective-permute-start.1 = (bf16[16,512]{1,0:T(8,128)(2,1)}, bf16[16,512]{1,0:T(8,128)(2,1)}, u32[]{:S(2)}, u32[]{:S(2)}) collective-permute-start(bf16[16,512]{1,0:T(8,128)(2,1)} %get-tuple-element.87), channel_id=1, source_target_pairs={{4,0},{8,4},{12,8},{5,1},{9,5},{13,9},{6,2},{10,6},{14,10},{7,3},{... | collective-permute-start | bytes 49160 | tf_op jit(solution)/shard_map/ppermute | solution.py:24
  2.6 14.9 %collective-permute-start = (bf16[16,512]{1,0:T(8,128)(2,1)}, bf16[16,512]{1,0:T(8,128)(2,1)}, u32[]{:S(2)}, u32[]{:S(2)}) collective-permute-start(bf16[16,512]{1,0:T(8,128)(2,1)} %get-tuple-element.88), channel_id=1, source_target_pairs={{0,4},{4,8},{8,12},{1,5},{5,9},{9,13},{2,6},{6,10},{10,14},{3,7},{... | collective-permute-start | bytes 49160 | tf_op jit(solution)/shard_map/ppermute | solution.py:22
  14.4 3.9 %copy-start.2 = (bf16[256,512]{1,0:T(8,128)(2,1)S(1)}, bf16[256,512]{1,0:T(8,128)(2,1)}, u32[]{:S(2)}) copy-start(bf16[256,512]{1,0:T(8,128)(2,1)} %param.7) | copy-start | bytes 786436
  19.7 5.7 %collective-permute-start.2 = (bf16[256,127]{1,0:T(8,128)(2,1)S(1)}, bf16[256,127]{1,0:T(8,128)(2,1)S(1)}, u32[]{:S(2)}, u32[]{:S(2)}) collective-permute-start(bf16[256,127]{1,0:T(8,128)(2,1)S(1)} %get-tuple-element.85), channel_id=1, source_target_pairs={{0,2},{1,3},{4,6},{5,7},{8,10},{9,11},{12,14},{13,15},{16,18},{17,... | collective-permute-start | bytes 195080 | tf_op jit(solution)/shard_map/ppermute | solution.py:22
  23.6 6.2 %collective-permute-start.3 = (bf16[256,127]{1,0:T(8,128)(2,1)S(1)}, bf16[256,127]{1,0:T(8,128)(2,1)S(1)}, u32[]{:S(2)}, u32[]{:S(2)}) collective-permute-start(bf16[256,127]{1,0:T(8,128)(2,1)S(1)} %get-tuple-element.86), channel_id=1, source_target_pairs={{2,0},{3,1},{6,4},{7,5},{10,8},{11,9},{14,12},{15,13},{18,16},{19,... | collective-permute-start | bytes 195080 | tf_op jit(solution)/shard_map/ppermute | solution.py:24
  31.2 7.8 %all-to-all-start.1 = ((bf16[2,64,512]{2,1,0:T(8,128)(2,1)}), bf16[2,64,512]{2,1,0:T(8,128)(2,1)S(1)}, u32[]{:S(2)}, u32[]{:S(2)}) async-start(bf16[2,64,512]{2,1,0:T(8,128)(2,1)} %bitcast.15), calls=%async_computation.1 | async-start | bytes 262144 | tf_op jit(solution)/shard_map/all_to_all | solution.py:126
  35.1 9.3 %copy-start.3 = (s32[1,64,64]{2,1,0:T(8,128)S(1)}, s32[1,64,64]{2,1,0:T(8,128)}, u32[]{:S(2)}) copy-start(s32[1,64,64]{2,1,0:T(8,128)} %param.11) | copy-start | bytes 49156
  40.2 26.7 %all-to-all-start = ((bf16[8,128,512]{1,2,0:T(8,128)(2,1)}), bf16[8,128,512]{1,2,0:T(8,128)(2,1)S(1)}, u32[]{:S(2)}, u32[]{:S(2)}) async-start(bf16[8,128,512]{1,2,0:T(8,128)(2,1)} %bitcast.9), calls=%async_computation | async-start | bytes 2097152 | tf_op jit(solution)/shard_map/all_to_all | solution.py:120
  108.5 1.4 copy-start
  108.5 2.0 copy-start.1
  110.5 1.7 slice-start
  129.4 1.4 copy-start
  129.4 2.0 copy-start.1
  131.4 1.7 slice-start
  150.3 1.4 copy-start
  150.3 2.0 copy-start.1
  152.4 1.7 slice-start
  171.3 1.4 copy-start
  171.3 2.0 copy-start.1
  173.3 1.7 slice-start
  192.2 1.4 copy-start
  192.2 2.0 copy-start.1
  194.2 1.7 slice-start
  213.1 1.4 copy-start
  213.1 2.0 copy-start.1
  215.1 1.7 slice-start
  234.0 1.4 copy-start
  234.0 2.0 copy-start.1
  236.0 1.7 slice-start
  254.9 1.4 copy-start
  254.9 2.0 copy-start.1
  256.9 1.7 slice-start
where the time goes:
time: 270 us; the launch traced here: 268 us
  local copies, waits for them, and re-layouts  183 us (68%)
  waiting for transfers between devices  30.3 us (11%)
  starting transfers between devices  19.8 us (7%)
  matrix products  17.7 us (7%)
  other arithmetic  15.9 us (6%)
    while x40, local copies, waits for them, and re-layouts  57.8 us
    another operation x20, local copies, waits for them, and re-layouts, band_matrix(): repeated = jnp.tile(padded, row_count)[:row_count * col_count]  36.9 us
    gather x2, local copies, waits for them, and re-layouts, per_device(): energy_partner = jnp.take(energy_buffer, row_index)  25.8 us
    all_to_all x1, waiting for transfers between devices, per_device(): lax.all_to_all(spread_out, ('tap', 'tm'), split_axis=0, concat_axis=2, ti...  21.9 us
    gather x8, local copies, waits for them, and re-layouts, lag_products(): picked = jnp.take(buffer, row_index, axis=0)  16.5 us
    dot_general x8, matrix products, lag_products(): lax.dot_general(shifted, toeplitz, (((1,), (1,)), ((), ())), preferred_el...  15.8 us
    ppermute x2, starting transfers between devices, extended(): lax.ppermute(tail, axis, [(i, (i + 1) % count) for i in range(ends)])  10 us
    select_n x16, other arithmetic, lag_products(): picked = jnp.take(buffer, row_index, axis=0)  9.78 us
  transfers between devices with their start and end apart: 6, of which 4 were waited for; matrix products, arithmetic and copies ran while one was open for 4% of the time, Pallas kernels for 0%

commit v1 on v0

v1 whole, which is shorter than its diff:
```python
import jax
import jax.numpy as jnp
from jax import lax
from jax.experimental import pallas as pl
from jax.experimental.pallas import tpu as pltpu
from jax.sharding import PartitionSpec as P

LAG_COUNT = 512
EPSILON = 1e-06
HALO = 16
TILE = 256
LANES = 128
GROUP = 8


def split_parts(matrix):
    high_part = matrix.astype(jnp.bfloat16)
    low_part = (matrix - high_part.astype(jnp.float32)).astype(jnp.bfloat16)
    return high_part, low_part


def shifted_rows(row, row_count):
    wide = jnp.broadcast_to(row, (row_count, row.shape[1]))
    return pltpu.roll(wide, 0, 1, stride=1, stride_axis=0)


def gathered(raw):
    lag_devices = lax.axis_size("lag")
    half_rows = raw.shape[0] // lag_devices
    half = lax.dynamic_slice_in_dim(raw, lax.axis_index("lag") * half_rows, half_rows, 0)

    def shifted(cells, axis, step):
        count = lax.axis_size(axis)
        return lax.ppermute(cells, axis, [(i, (i + step) % count) for i in range(count)])

    times = [half] + [shifted(half, "tm", step) for step in range(1, lax.axis_size("tm"))]
    taps = [jnp.stack(times)]
    for step in range(1, lax.axis_size("tap")):
        taps.append(jnp.stack([shifted(cells, "tap", step) for cells in times]))
    cable = jnp.stack(taps)
    return jnp.stack([cable] + [shifted(cable, "lag", step) for step in range(1, lag_devices)])


def correlate_body(
    table_ref, chosen_ref, space_ref, time_ref, cable_ref, out_ref,
    raw_ref, smooth_ref, bank_ref, flip_ref, scale_ref, picked_ref, sems,
    *, lag_devices, block_taps, time_step, dest_count, source_count, partner_count
):
    tap_devices, time_devices = cable_ref.shape[1], cable_ref.shape[2]
    time_total = time_devices * time_step
    block_total = tap_devices * lag_devices
    ext_rows = block_taps + 2 * HALO
    segments = dest_count + 1
    step_id = pl.program_id(0)
    tap_index = table_ref[segments]
    time_index = table_ref[segments + 1]
    lag_index = table_ref[segments + 2]

    def pieces(segment):
        block = table_ref[segment]
        for part, (block_at, source, target, size) in enumerate((
            (jnp.maximum(block - 1, 0), block_taps - HALO, 0, HALO),
            (block, 0, HALO, block_taps),
            (jnp.minimum(block + 1, block_total - 1), 0, HALO + block_taps, HALO),
        )):
            lag_step = lax.rem(lag_index - lax.rem(block_at, lag_devices) + lag_devices, lag_devices)
            tap_step = lax.rem(tap_index - lax.div(block_at, lag_devices) + tap_devices, tap_devices)
            for time_at in range(time_devices):
                time_step_back = lax.rem(time_index - time_at + time_devices, time_devices)
                yield pltpu.make_async_copy(
                    cable_ref.at[lag_step, tap_step, time_step_back, pl.ds(source, size)],
                    raw_ref.at[segment, pl.ds(target, size), pl.ds(time_at * time_step, time_step)],
                    sems.at[segment, part * time_devices + time_at],
                )

    @pl.when(step_id == 0)
    def prepare():
        for segment in range(segments):
            for piece in pieces(segment):
                piece.start()
        rows_at = lax.broadcasted_iota(jnp.int32, (block_taps, TILE), 1)
        space_wide = shifted_rows(space_ref[...], block_taps)[:, :ext_rows]
        time_wide = shifted_rows(time_ref[...], TILE)
        time_high, time_low = split_parts(time_wide)
        smooth_ref[:, :LANES] = jnp.zeros((segments * block_taps, LANES), jnp.bfloat16)
        smooth_ref[:, pl.ds(LANES + time_total, LANES)] = jnp.zeros(
            (segments * block_taps, LANES), jnp.bfloat16
        )
        rows_at = rows_at[:, :ext_rows]
        for segment in range(segments):
            for piece in pieces(segment):
                piece.wait()
            block = table_ref[segment]
            first = jnp.where(block == 0, HALO, 0)
            last = jnp.where(block == block_total - 1, HALO + block_taps, ext_rows)
            inside = jnp.logical_and(rows_at >= first, rows_at < last)
            space_high, space_low = split_parts(jnp.where(inside, space_wide, 0.0))
            strain = raw_ref[segment]
            smooth = jnp.dot(space_high, strain, preferred_element_type=jnp.float32)
            smooth = smooth + jnp.dot(space_low, strain, preferred_element_type=jnp.float32)
            smooth_ref[
                segment * block_taps : (segment + 1) * block_taps, pl.ds(LANES, time_total)
            ] = smooth.astype(jnp.bfloat16)
        transposed = (((1,), (1,)), ((), ()))
        dest_rows = dest_count * block_taps
        power = jnp.zeros((segments * block_taps, 1), jnp.float32)
        for tile in range(time_total // TILE):
            window = smooth_ref[:, tile * TILE : tile * TILE + 2 * TILE]
            white = lax.dot_general(
                window, time_high, transposed, preferred_element_type=jnp.float32
            )
            white = white + lax.dot_general(
                window, time_low, transposed, preferred_element_type=jnp.float32
            )
            white = white.astype(jnp.bfloat16)
            bank_ref[:, tile * TILE : (tile + 1) * TILE] = white
            white = white.astype(jnp.float32)
            power = power + jnp.sum(white * white, axis=1, keepdims=True)
        energy = power / time_total + EPSILON
        inverse = jnp.broadcast_to(1.0 / jnp.sqrt(energy), (segments * block_taps, LANES))
        inverse_high, inverse_low = split_parts(inverse)
        bank_ref[:, pl.ds(time_total, LANES)] = inverse_high
        bank_ref[:, pl.ds(time_total + LANES, LANES)] = inverse_low
        scale_ref[...] = inverse[dest_rows:]
        at_row = lax.broadcasted_iota(jnp.int32, (2 * TILE, TILE), 0)
        at_col = lax.broadcasted_iota(jnp.int32, (2 * TILE, TILE), 1)
        mirror = (at_row + at_col == TILE).astype(jnp.bfloat16)
        flip_ref[:, :LANES] = jnp.zeros((block_taps, LANES), jnp.float32)
        blank = jnp.zeros((block_taps, TILE), jnp.bfloat16)
        tiles = time_total // TILE
        for tile in range(tiles + 1):
            upper = bank_ref[dest_rows:, pl.ds((tiles - tile) * TILE, TILE)] if tile else blank
            lower = bank_ref[dest_rows:, pl.ds((tiles - tile - 1) * TILE, TILE)] if tile < tiles else blank
            turned = jnp.dot(
                jnp.concatenate([lower, upper], axis=1), mirror, preferred_element_type=jnp.float32
            )
            width = TILE if tile < tiles else LANES
            flip_ref[:, pl.ds(LANES + tile * TILE, width)] = turned[:, :width]

    dest_rows = dest_count * block_taps
    picked = jnp.dot(chosen_ref[...], bank_ref[:dest_rows, :], preferred_element_type=jnp.float32)
    picked_ref[...] = picked[:, :time_total].astype(jnp.bfloat16)
    partner_scale = picked[:, time_total : time_total + LANES] + picked[:, time_total + LANES :]
    blank = jnp.zeros((LANES, LANES), jnp.bfloat16)
    edge = jnp.zeros((partner_count, TILE), jnp.bfloat16)
    lag_tiles = LAG_COUNT // TILE
    window_scale = 1.0 / (float(time_total) ** 0.5)
    first_row = time_index * source_count + step_id * GROUP
    for member in range(GROUP):
        row = flip_ref[pl.ds(first_row + member, 1), :]
        wide = shifted_rows(row, LANES).astype(jnp.bfloat16)

        def diagonal(k):
            if k < 0 or k > time_total // LANES:
                return blank
            start = time_total + LANES - LANES * k
            return wide[:, start : start + LANES]

        weights = jnp.concatenate(
            [
                jnp.concatenate([diagonal(k), diagonal(k - 1)], axis=1)
                for k in range(2 * (time_total // TILE + lag_tiles - 1))
            ],
            axis=0,
        )
        rows = picked_ref[member * partner_count : (member + 1) * partner_count, :]
        stacked = jnp.concatenate(
            [
                jnp.concatenate([edge] * (lag_tiles - 1 - j) + [rows] + [edge] * j, axis=1)
                for j in range(lag_tiles)
            ],
            axis=0,
        )
        products = jnp.dot(stacked, weights, preferred_element_type=jnp.float32)
        scale = partner_scale[member * partner_count : (member + 1) * partner_count, :]
        scale = scale * scale_ref[pl.ds(first_row + member, 1), :] * window_scale
        scale = jnp.concatenate([scale, scale], axis=1)
        for j in range(lag_tiles):
            part = products[j * partner_count : (j + 1) * partner_count] * scale
            out_ref[0, member, :, j * TILE : (j + 1) * TILE] = part.astype(jnp.bfloat16)


def per_device(raw_strain, spatial_filter, temporal_filter, dest_blocks, partner_codes):
    taps_here, time_step = raw_strain.shape
    lag_devices = lax.axis_size("lag")
    tap_devices = lax.axis_size("tap")
    time_devices = lax.axis_size("tm")
    time_total = time_step * time_devices
    block_taps = taps_here // lag_devices
    dest_count = dest_blocks.shape[1]
    _, source_count, partner_count = partner_codes.shape
    segments = dest_count + 1
    tap_index = lax.axis_index("tap")
    time_index = lax.axis_index("tm")
    lag_index = lax.axis_index("lag")
    block_here = tap_index * lag_devices + lag_index
    cable = gathered(raw_strain)
    table = jnp.concatenate(
        [
            lax.dynamic_index_in_dim(dest_blocks, block_here, 0, keepdims=False),
            jnp.stack([block_here, tap_index, time_index, lag_index]).astype(jnp.int32),
        ]
    )
    dest_rows = dest_count * block_taps
    codes = partner_codes.reshape(source_count * partner_count, 1)
    chosen = (codes == jnp.arange(dest_rows, dtype=jnp.int32)[None, :]).astype(jnp.bfloat16)
    space_row = jnp.pad(spatial_filter, (0, TILE - spatial_filter.shape[0]))[None, :]
    time_row = jnp.pad(
        temporal_filter, (1, 2 * TILE - 1 - temporal_filter.shape[0])
    )[None, :]
    rows_all = segments * block_taps
    body = lambda *refs: correlate_body(
        *refs, lag_devices=lag_devices, block_taps=block_taps, time_step=time_step,
        dest_count=dest_count, source_count=source_count, partner_count=partner_count,
    )
    return pl.pallas_call(
        body,
        grid_spec=pltpu.PrefetchScalarGridSpec(
            num_scalar_prefetch=1,
            grid=(source_count // GROUP,),
            in_specs=[
                pl.BlockSpec((GROUP * partner_count, dest_rows), lambda i, t: (i, 0)),
                pl.BlockSpec((1, TILE), lambda i, t: (0, 0)),
                pl.BlockSpec((1, 2 * TILE), lambda i, t: (0, 0)),
                pl.BlockSpec(memory_space=pl.ANY),
            ],
            out_specs=pl.BlockSpec((1, GROUP, partner_count, LAG_COUNT), lambda i, t: (0, i, 0, 0)),
            scratch_shapes=[
                pltpu.VMEM((segments, block_taps + 2 * HALO, time_total), jnp.bfloat16),
                pltpu.VMEM((rows_all, time_total + 2 * LANES), jnp.bfloat16),
                pltpu.VMEM((rows_all, time_total + 2 * LANES), jnp.bfloat16),
                pltpu.VMEM((block_taps, time_total + 2 * LANES), jnp.float32),
                pltpu.VMEM((block_taps, LANES), jnp.float32),
                pltpu.VMEM((GROUP * partner_count, time_total), jnp.bfloat16),
                pltpu.SemaphoreType.DMA((segments, 3 * time_devices)),
            ],
        ),
        out_shape=jax.ShapeDtypeStruct((1, source_count, partner_count, LAG_COUNT), jnp.bfloat16),
        compiler_params=pltpu.CompilerParams(vmem_limit_bytes=56 << 20),
    )(table, chosen, space_row, time_row, cable)


def solution(mesh):
    placed = (
        P(("groups", "tap"), "tm"),
        P(),
        P(),
        P("groups", None),
        P(("groups", "tap", "lag"), "tm", None),
    )
    return jax.shard_map(
        per_device,
        mesh=mesh,
        in_specs=placed,
        out_specs=P(("groups", "tap", "lag"), "tm", None, None),
        check_vma=False,
    )
```

time: 270 us -> 51.3 us (0.19)
  local copies, waits for them, and re-layouts: 183 us -> 3.42 us
  matrix products: 17.7 us -> 0 us
  Pallas kernels: 0 us -> 16.6 us
  waiting for transfers between devices: 30.3 us -> 15.9 us
  other arithmetic: 15.9 us -> 3.47 us
  starting transfers between devices: 19.8 us -> 11 us
    while x40 -> x0, local copies, waits for them, and re-layouts: 57.8 us -> none
    gather x13 -> x0, local copies, waits for them, and re-layouts: 43.6 us -> none  [the longest x2 25.8 us: per_device(): energy_partner = jnp.take(energy_buffer, row_index)]
    another operation x20 -> x1, local copies, waits for them, and re-layouts: 36.9 us -> 0.01 us  [gathered(): taps = [jnp.stack(times)]]
    all_to_all x2 -> x0, waiting for transfers between devices: 25.4 us -> none  [the longest x1 21.9 us: per_device(): lax.all_to_all(spread_out, ('tap', 'tm'), split_axis=0, concat_axis=2, ti...]
    dot_general x13 -> x0, matrix products: 17.7 us -> none  [the longest x8 15.8 us: lag_products(): lax.dot_general(shifted, toeplitz, (((1,), (1,)), ((), ())), preferred_el...]
    pallas_call x0 -> x1, Pallas kernels: none -> 16.6 us  [per_device(): pl.pallas_call(body, grid_spec=pltpu.PrefetchScalarGridSpec(num_scalar_pr...]
    slice x28 -> x0, local copies, waits for them, and re-layouts: 16 us -> none  [the longest x18 9.48 us: band_matrix(): repeated = jnp.tile(padded, row_count)[:row_count * col_count]]
    ppermute x4 -> x8, waiting for transfers between devices: 4.85 us -> 15.9 us  [shifted(): lax.ppermute(cells, axis, [(i, (i + step) % count) for i in range(count)])]
  transfers between devices with their start and end apart: 6 -> 8, of which waited for: 4 -> 2; matrix products, arithmetic and copies ran while one was open for 4% -> 8% of each run, Pallas kernels for 0% -> 0%
where the time goes in v1:
time: 51.3 us; the launch traced here: 50.5 us
  Pallas kernels  16.6 us (32%)
  waiting for transfers between devices  15.9 us (31%)
  starting transfers between devices  11 us (21%)
  other arithmetic  3.47 us (7%)
  local copies, waits for them, and re-layouts  3.42 us (7%)
    pallas_call x1, Pallas kernels, per_device(): pl.pallas_call(body, grid_spec=pltpu.PrefetchScalarGridSpec(num_scalar_pr...  16.6 us
    ppermute x8, waiting for transfers between devices, shifted(): lax.ppermute(cells, axis, [(i, (i + step) % count) for i in range(count)])  15.9 us
    ppermute x8, starting transfers between devices, shifted(): lax.ppermute(cells, axis, [(i, (i + step) % count) for i in range(count)])  11 us
    convert_element_type x1, other arithmetic, per_device(): (codes == jnp.arange(dest_rows, dtype=jnp.int32)[None, :]).astype(jnp.bfl...  1.69 us
    another operation x2, other arithmetic, gathered(): jnp.stack([cable] + [shifted(cable, 'lag', step) for step in range(1, lag...  1.67 us
    unnamed x10, local copies, waits for them, and re-layouts  1.22 us
  transfers between devices with their start and end apart: 8, of which 2 were waited for; matrix products, arithmetic and copies ran while one was open for 8% of the time, Pallas kernels for 0%

profile of v1, /device:TPU:0, one launch (start us, length us, event | category | flops | bytes accessed | tf_op | source)
XLA Modules:
  0.0 50.5 jit_solution(17407257208112768633)
XLA Ops:
  0.0 0.0 copy-start
  0.0 0.9 %copy-done = bf16[256,512]{1,0:T(8,128)(2,1)S(1)} copy-done((bf16[256,512]{1,0:T(8,128)(2,1)S(1)}, bf16[256,512]{1,0:T(8,128)(2,1)}, u32[]{:S(2)}) %copy-start) | copy-done | bytes 262168
  1.0 3.0 %collective-permute-start = (bf16[128,512]{1,0:T(8,128)(2,1)S(1)}, bf16[128,512]{1,0:T(8,128)(2,1)S(1)}, u32[]{:S(2)}, u32[]{:S(2)}) collective-permute-start(bf16[128,512]{1,0:T(8,128)(2,1)S(1)} %constant_dynamic-slice_fusion), channel_id=1, source_target_pairs={{0,2},{2,0},{1,3},{3,1},{4,6},{6,4},{5,7},{7,5},{8,10},{10,8},{9,1... | collective-permute-start | bytes 393224 | tf_op jit(solution)/shard_map/ppermute | solution.py:34
  4.0 2.6 %collective-permute-start.3 = (bf16[128,512]{1,0:T(8,128)(2,1)S(1)}, bf16[128,512]{1,0:T(8,128)(2,1)S(1)}, u32[]{:S(2)}, u32[]{:S(2)}) collective-permute-start(bf16[128,512]{1,0:T(8,128)(2,1)S(1)} %constant_dynamic-slice_fusion), channel_id=1, source_target_pairs={{0,8},{4,12},{8,0},{12,4},{1,9},{5,13},{9,1},{13,5},{2,10},{6,14},... | collective-permute-start | bytes 393224 | tf_op jit(solution)/shard_map/ppermute | solution.py:34
  6.6 1.6 %collective-permute-start.1 = (bf16[128,512]{1,0:T(8,128)(2,1)S(1)}, bf16[128,512]{1,0:T(8,128)(2,1)S(1)}, u32[]{:S(2)}, u32[]{:S(2)}) collective-permute-start(bf16[128,512]{1,0:T(8,128)(2,1)S(1)} %constant_dynamic-slice_fusion), channel_id=1, source_target_pairs={{0,4},{4,8},{8,12},{12,0},{1,5},{5,9},{9,13},{13,1},{2,6},{6,10},{... | collective-permute-start | bytes 393224 | tf_op jit(solution)/shard_map/ppermute | solution.py:34
  8.1 2.2 %collective-permute-start.5 = (bf16[128,512]{1,0:T(8,128)(2,1)S(1)}, bf16[128,512]{1,0:T(8,128)(2,1)S(1)}, u32[]{:S(2)}, u32[]{:S(2)}) collective-permute-start(bf16[128,512]{1,0:T(8,128)(2,1)S(1)} %constant_dynamic-slice_fusion), channel_id=1, source_target_pairs={{0,12},{4,0},{8,4},{12,8},{1,13},{5,1},{9,5},{13,9},{2,14},{6,2},{... | collective-permute-start | bytes 393224 | tf_op jit(solution)/shard_map/ppermute | solution.py:34
  10.4 0.0 collective-permute-done
  10.4 0.0 collective-permute-start.4
  10.4 1.5 %collective-permute-start.2 = (bf16[128,512]{1,0:T(8,128)(2,1)S(1)}, bf16[128,512]{1,0:T(8,128)(2,1)S(1)}, u32[]{:S(2)}, u32[]{:S(2)}) collective-permute-start(bf16[128,512]{1,0:T(8,128)(2,1)S(1)} %collective-permute-done), channel_id=1, source_target_pairs={{0,4},{4,8},{8,12},{12,0},{1,5},{5,9},{9,13},{13,1},{2,6},{6,10},{... | collective-permute-start | bytes 393224 | tf_op jit(solution)/shard_map/ppermute | solution.py:34
  12.0 9.2 %collective-permute-done.3 = bf16[128,512]{1,0:T(8,128)(2,1)S(1)} collective-permute-done((bf16[128,512]{1,0:T(8,128)(2,1)S(1)}, bf16[128,512]{1,0:T(8,128)(2,1)S(1)}, u32[]{:S(2)}, u32[]{:S(2)}) %collective-permute-start.3) | collective-permute-done | bytes 131104 | tf_op jit(solution)/shard_map/ppermute | solution.py:34
  21.2 0.0 collective-permute-start.6
  21.2 6.7 %collective-permute-done.4 = bf16[128,512]{1,0:T(8,128)(2,1)S(1)} collective-permute-done((bf16[128,512]{1,0:T(8,128)(2,1)S(1)}, bf16[128,512]{1,0:T(8,128)(2,1)S(1)}, u32[]{:S(2)}, u32[]{:S(2)}) %collective-permute-start.4) | collective-permute-done | bytes 131104 | tf_op jit(solution)/shard_map/ppermute | solution.py:34
  27.9 0.0 collective-permute-done.1
  27.9 0.0 collective-permute-done.2
  27.9 0.0 copy-start.4
  27.9 0.0 copy-start.2
  27.9 0.0 copy-start.1
  27.9 0.0 copy-start.3
  28.0 0.0 collective-permute-done.5
  28.0 0.0 collective-permute-done.6
  28.0 0.2 fusion.1
  28.2 0.1 collective-permute-start.7
  28.3 0.2 copy-done.4
  28.6 0.6 %pad.8 = f32[256]{0:T(256)} pad(f32[33]{0:T(128)S(1)} %copy-done.4, f32[]{:T(128)} %constant.23.clone.1), padding=0_223 | pad | bytes 1160 | tf_op jit(solution)/shard_map/jit(_pad)/pad | solution.py:207
  29.2 0.7 %pad.9 = f32[512]{0:T(512)} pad(f32[255]{0:T(256)S(1)} %copy-done.2, f32[]{:T(128)} %constant.23.clone.1), padding=1_256 | pad | bytes 3072 | tf_op jit(solution)/shard_map/jit(_pad)/pad | solution.py:208
  29.8 0.1 eq.15
  29.9 0.2 dynamic-slice_reduce_fusion
  30.1 0.7 %concatenate.3.refs_0_ = s32[6]{0:T(128)} concatenate(s32[2]{0:T(128)S(1)} %dynamic-slice_reduce_fusion, s32[1]{0:T(128)} %bitcast, s32[1]{0:T(128)} %bitcast.1, s32[1]{0:T(128)} %bitcast.2, s32[1]{0:T(128)} %bitcast.3), dimensions={0} | concatenate | bytes 48 | tf_op jit(solution)/shard_map/concatenate | solution.py:198
  30.7 1.7 %fusion.refs_1_ = bf16[4096,256]{1,0:T(8,128)(2,1)} fusion(s32[4096]{0:T(1024)S(1)} %eq.15), kind=kLoop, calls=%fused_computation.1 | loop fusion | flops 2097152 | bytes 2113536 | tf_op jit(solution)/shard_map/convert_element_type | solution.py:206
  32.4 0.0 collective-permute-done.7
  32.4 1.5 %pad_maximum_fusion.refs_4_ = bf16[2,4,2,128,512]{4,3,2,1,0:T(8,128)(2,1)} fusion(bf16[1,4,2,128,512]{4,3,2,1,0:T(8,128)(2,1)S(1)} %bitcast.26, bf16[1,4,2,128,512]{4,3,2,1,0:T(8,128)(2,1)S(1)} %get-tuple-element.5), kind=kLoop, calls=%fused_computation.2 | loop fusion | flops 1048576 | bytes 4194304 | tf_op jit(solution)/shard_map/stack | solution.py:41
  33.9 16.6 %shard_map.55 = bf16[1,64,64,512]{3,2,1,0:T(8,128)(2,1)} custom-call(s32[6]{0:T(128)} %concatenate.3.refs_0_, bf16[4096,256]{1,0:T(8,128)(2,1)} %fusion.refs_1_, f32[1,256]{1,0:T(1,128)} %bitcast.35, f32[1,512]{1,0:T(1,128)} %bitcast.34, bf16[2,4,2,128,512]{4,3,2,1,0:T(8,128)(2,1)} %pad_maximum_fusion.refs_4_), custom_call_target="tpu_custom_call" | custom-call | tf_op jit(solution)/shard_map/pallas_call | solution.py:216
  (9 shorter events, 0.1 us)
Async XLA Ops:
  0.0 1.0 %copy-start = (bf16[256,512]{1,0:T(8,128)(2,1)S(1)}, bf16[256,512]{1,0:T(8,128)(2,1)}, u32[]{:S(2)}) copy-start(bf16[256,512]{1,0:T(8,128)(2,1)} %param.5) | copy-start | bytes 786436
  1.0 9.4 %collective-permute-start = (bf16[128,512]{1,0:T(8,128)(2,1)S(1)}, bf16[128,512]{1,0:T(8,128)(2,1)S(1)}, u32[]{:S(2)}, u32[]{:S(2)}) collective-permute-start(bf16[128,512]{1,0:T(8,128)(2,1)S(1)} %constant_dynamic-slice_fusion), channel_id=1, source_target_pairs={{0,2},{2,0},{1,3},{3,1},{4,6},{6,4},{5,7},{7,5},{8,10},{10,8},{9,1... | collective-permute-start | bytes 393224 | tf_op jit(solution)/shard_map/ppermute | solution.py:34
  4.0 17.2 %collective-permute-start.3 = (bf16[128,512]{1,0:T(8,128)(2,1)S(1)}, bf16[128,512]{1,0:T(8,128)(2,1)S(1)}, u32[]{:S(2)}, u32[]{:S(2)}) collective-permute-start(bf16[128,512]{1,0:T(8,128)(2,1)S(1)} %constant_dynamic-slice_fusion), channel_id=1, source_target_pairs={{0,8},{4,12},{8,0},{12,4},{1,9},{5,13},{9,1},{13,5},{2,10},{6,14},... | collective-permute-start | bytes 393224 | tf_op jit(solution)/shard_map/ppermute | solution.py:34
  6.6 21.3 %collective-permute-start.1 = (bf16[128,512]{1,0:T(8,128)(2,1)S(1)}, bf16[128,512]{1,0:T(8,128)(2,1)S(1)}, u32[]{:S(2)}, u32[]{:S(2)}) collective-permute-start(bf16[128,512]{1,0:T(8,128)(2,1)S(1)} %constant_dynamic-slice_fusion), channel_id=1, source_target_pairs={{0,4},{4,8},{8,12},{12,0},{1,5},{5,9},{9,13},{13,1},{2,6},{6,10},{... | collective-permute-start | bytes 393224 | tf_op jit(solution)/shard_map/ppermute | solution.py:34
  8.1 19.8 %collective-permute-start.5 = (bf16[128,512]{1,0:T(8,128)(2,1)S(1)}, bf16[128,512]{1,0:T(8,128)(2,1)S(1)}, u32[]{:S(2)}, u32[]{:S(2)}) collective-permute-start(bf16[128,512]{1,0:T(8,128)(2,1)S(1)} %constant_dynamic-slice_fusion), channel_id=1, source_target_pairs={{0,12},{4,0},{8,4},{12,8},{1,13},{5,1},{9,5},{13,9},{2,14},{6,2},{... | collective-permute-start | bytes 393224 | tf_op jit(solution)/shard_map/ppermute | solution.py:34
  10.4 17.5 %collective-permute-start.4 = (bf16[128,512]{1,0:T(8,128)(2,1)S(1)}, bf16[128,512]{1,0:T(8,128)(2,1)S(1)}, u32[]{:S(2)}, u32[]{:S(2)}) collective-permute-start(bf16[128,512]{1,0:T(8,128)(2,1)S(1)} %collective-permute-done), channel_id=1, source_target_pairs={{0,8},{4,12},{8,0},{12,4},{1,9},{5,13},{9,1},{13,5},{2,10},{6,14},... | collective-permute-start | bytes 393224 | tf_op jit(solution)/shard_map/ppermute | solution.py:34
  10.4 17.5 %collective-permute-start.2 = (bf16[128,512]{1,0:T(8,128)(2,1)S(1)}, bf16[128,512]{1,0:T(8,128)(2,1)S(1)}, u32[]{:S(2)}, u32[]{:S(2)}) collective-permute-start(bf16[128,512]{1,0:T(8,128)(2,1)S(1)} %collective-permute-done), channel_id=1, source_target_pairs={{0,4},{4,8},{8,12},{12,0},{1,5},{5,9},{9,13},{13,1},{2,6},{6,10},{... | collective-permute-start | bytes 393224 | tf_op jit(solution)/shard_map/ppermute | solution.py:34
  21.2 6.8 %collective-permute-start.6 = (bf16[128,512]{1,0:T(8,128)(2,1)S(1)}, bf16[128,512]{1,0:T(8,128)(2,1)S(1)}, u32[]{:S(2)}, u32[]{:S(2)}) collective-permute-start(bf16[128,512]{1,0:T(8,128)(2,1)S(1)} %collective-permute-done), channel_id=1, source_target_pairs={{0,12},{4,0},{8,4},{12,8},{1,13},{5,1},{9,5},{13,9},{2,14},{6,2},{... | collective-permute-start | bytes 393224 | tf_op jit(solution)/shard_map/ppermute | solution.py:34
  27.9 0.7 %copy-start.4 = (f32[33]{0:T(128)S(1)}, f32[33]{0:T(128)}, u32[]{:S(2)}) copy-start(f32[33]{0:T(128)} %param.6) | copy-start | bytes 400
  27.9 1.2 %copy-start.2 = (f32[255]{0:T(256)S(1)}, f32[255]{0:T(256)}, u32[]{:S(2)}) copy-start(f32[255]{0:T(256)} %param.7) | copy-start | bytes 3064
  27.9 1.9 %copy-start.1 = (s32[1,64,64]{2,1,0:T(8,128)S(1)}, s32[1,64,64]{2,1,0:T(8,128)}, u32[]{:S(2)}) copy-start(s32[1,64,64]{2,1,0:T(8,128)} %param.9) | copy-start | bytes 49156
  27.9 2.0 %copy-start.3 = (s32[8,2]{0,1:T(2,128)S(1)}, s32[8,2]{0,1:T(2,128)}, u32[]{:S(2)}) copy-start(s32[8,2]{0,1:T(2,128)} %param.8) | copy-start | bytes 196
  28.2 4.2 %collective-permute-start.7 = (bf16[4,2,128,512]{3,2,1,0:T(8,128)(2,1)S(1)}, bf16[4,2,128,512]{3,2,1,0:T(8,128)(2,1)S(1)}, u32[]{:S(2)}, u32[]{:S(2)}) collective-permute-start(bf16[4,2,128,512]{3,2,1,0:T(8,128)(2,1)S(1)} %get-tuple-element.6), channel_id=1, source_target_pairs={{0,1},{1,0},{2,3},{3,2},{4,5},{5,4},{6,7},{7,6},{8,9},{9,8},{10,11... | collective-permute-start | bytes 3145736 | tf_op jit(solution)/shard_map/ppermute | solution.py:34

commit v2 on v1

v2 whole, which is shorter than its diff:
```python
import functools

import jax
import jax.numpy as jnp
from jax import lax
from jax.experimental import pallas as pl
from jax.experimental.pallas import tpu as pltpu
from jax.sharding import PartitionSpec as P

LAG_COUNT = 512
EPSILON = 1e-06
HALO = 16
TILE = 256
LANES = 128
GROUP = 16


def split_parts(matrix):
    high_part = matrix.astype(jnp.bfloat16)
    low_part = (matrix - high_part.astype(jnp.float32)).astype(jnp.bfloat16)
    return high_part, low_part


def shifted_rows(row, row_count):
    wide = jnp.broadcast_to(row, (row_count, row.shape[1]))
    return pltpu.roll(wide, 0, 1, stride=1, stride_axis=0)


def gathered(raw):
    lag_devices = lax.axis_size("lag")
    half_rows = raw.shape[0] // lag_devices
    half = lax.dynamic_slice_in_dim(raw, lax.axis_index("lag") * half_rows, half_rows, 0)

    def shifted(cells, axis, step):
        count = lax.axis_size(axis)
        return lax.ppermute(cells, axis, [(i, (i + step) % count) for i in range(count)])

    taps = [half] + [shifted(half, "tap", step) for step in range(1, lax.axis_size("tap"))]
    mine = [jnp.stack(taps)]
    for step in range(1, lax.axis_size("tm")):
        mine.append(jnp.stack([shifted(cells, "tm", step) for cells in taps]))
    cables = list(mine)
    for step in range(1, lag_devices):
        cables += [shifted(cells, "lag", step) for cells in mine]
    return cables


def correlate_body(*refs, cable_count, lag_devices, time_devices):
    dest_ref, codes_ref, space_ref, time_ref = refs[:4]
    cable_refs = refs[4 : 4 + cable_count]
    out_ref, raw_ref, smooth_ref, bank_ref, flip_ref, scale_ref, code_ref, picked_ref, sems = refs[
        4 + cable_count :
    ]
    tap_devices, block_taps, time_step = cable_refs[0].shape
    _, source_count, partner_count = codes_ref.shape
    dest_count = dest_ref.shape[1]
    dest_rows = dest_count * block_taps
    time_total = time_devices * time_step
    tiles = time_total // TILE
    block_total = tap_devices * lag_devices
    ext_rows = block_taps + 2 * HALO
    rows_all = dest_rows + source_count
    step_id = pl.program_id(0)
    tap_index = lax.axis_index("tap")
    time_index = lax.axis_index("tm")
    lag_index = lax.axis_index("lag")
    block_here = tap_index * lag_devices + lag_index

    def pieces(segment, block):
        for part, (block_at, source, target, size) in enumerate((
            (jnp.maximum(block - 1, 0), block_taps - HALO, 0, HALO),
            (block, 0, HALO, block_taps),
            (jnp.minimum(block + 1, block_total - 1), 0, HALO + block_taps, HALO),
        )):
            lag_step = lax.rem(lag_index - lax.rem(block_at, lag_devices) + lag_devices, lag_devices)
            tap_step = lax.rem(tap_index - lax.div(block_at, lag_devices) + tap_devices, tap_devices)
            for time_at in range(time_devices):
                time_back = lax.rem(time_index - time_at + time_devices, time_devices)
                cable_at = lag_step * time_devices + time_back

                def copy_from(ref):
                    return pltpu.make_async_copy(
                        ref.at[tap_step, pl.ds(source, size)],
                        raw_ref.at[
                            segment, pl.ds(target, size), pl.ds(time_at * time_step, time_step)
                        ],
                        sems.at[segment, part * time_devices + time_at],
                    )

                yield cable_at, copy_from

    def start_all(segment, block):
        for cable_at, copy_from in pieces(segment, block):
            for i, ref in enumerate(cable_refs):
                pl.when(cable_at == i)(lambda ref=ref, copy_from=copy_from: copy_from(ref).start())

    def wait_all(segment, block):
        for _, copy_from in pieces(segment, block):
            copy_from(cable_refs[0]).wait()

    @pl.when(step_id == 0)
    def prepare():
        blocks = [dest_ref[block_here, j] for j in range(dest_count)] + [block_here]
        for segment, block in enumerate(blocks):
            start_all(segment, block)
        code_ref[:, :source_count] = codes_ref[0].astype(jnp.float32).T
        space_row = jnp.pad(space_ref[...][None, :], ((0, 0), (0, TILE - space_ref.shape[0])))
        time_row = jnp.pad(time_ref[...][None, :], ((0, 0), (1, 2 * TILE - 1 - time_ref.shape[0])))
        rows_at = lax.broadcasted_iota(jnp.int32, (block_taps, ext_rows), 1)
        space_wide = shifted_rows(space_row, block_taps)[:, :ext_rows]
        time_wide = shifted_rows(time_row, TILE)
        time_high, time_low = split_parts(time_wide)
        smooth_ref[:, :LANES] = jnp.zeros((rows_all, LANES), jnp.bfloat16)
        smooth_ref[:, pl.ds(LANES + time_total, LANES)] = jnp.zeros((rows_all, LANES), jnp.bfloat16)
        for segment, block in enumerate(blocks):
            wait_all(segment, block)
            first = jnp.where(block == 0, HALO, 0)
            last = jnp.where(block == block_total - 1, HALO + block_taps, ext_rows)
            inside = jnp.logical_and(rows_at >= first, rows_at < last)
            space_high, space_low = split_parts(jnp.where(inside, space_wide, 0.0))
            strain = raw_ref[segment]
            smooth = jnp.dot(space_high, strain, preferred_element_type=jnp.float32)
            smooth = smooth + jnp.dot(space_low, strain, preferred_element_type=jnp.float32)
            smooth = smooth.astype(jnp.bfloat16)
            if segment < dest_count:
                smooth_ref[
                    segment * block_taps : (segment + 1) * block_taps, pl.ds(LANES, time_total)
                ] = smooth
            else:
                for part in range(time_devices):
                    @pl.when(time_index == part)
                    def keep_own():
                        smooth_ref[dest_rows:, pl.ds(LANES, time_total)] = smooth[
                            part * source_count : (part + 1) * source_count
                        ]
        transposed = (((1,), (1,)), ((), ()))
        power = jnp.zeros((rows_all, 1), jnp.float32)
        for tile in range(tiles):
            window = smooth_ref[:, tile * TILE : tile * TILE + 2 * TILE]
            white = lax.dot_general(
                window, time_high, transposed, preferred_element_type=jnp.float32
            )
            white = white + lax.dot_general(
                window, time_low, transposed, preferred_element_type=jnp.float32
            )
            white = white.astype(jnp.bfloat16)
            bank_ref[:, tile * TILE : (tile + 1) * TILE] = white
            white = white.astype(jnp.float32)
            power = power + jnp.sum(white * white, axis=1, keepdims=True)
        energy = power / time_total + EPSILON
        inverse = jnp.broadcast_to(1.0 / jnp.sqrt(energy), (rows_all, LANES))
        inverse_high, inverse_low = split_parts(inverse)
        bank_ref[:, pl.ds(time_total, LANES)] = inverse_high
        bank_ref[:, pl.ds(time_total + LANES, LANES)] = inverse_low
        scale_ref[...] = inverse[dest_rows:]
        at_row = lax.broadcasted_iota(jnp.int32, (2 * TILE, TILE), 0)
        at_col = lax.broadcasted_iota(jnp.int32, (2 * TILE, TILE), 1)
        mirror = (at_row + at_col == TILE).astype(jnp.bfloat16)
        flip_ref[:, :LANES] = jnp.zeros((source_count, LANES), jnp.float32)
        blank = jnp.zeros((source_count, TILE), jnp.bfloat16)
        for tile in range(tiles + 1):
            upper = bank_ref[dest_rows:, pl.ds((tiles - tile) * TILE, TILE)] if tile else blank
            lower = bank_ref[dest_rows:, pl.ds((tiles - tile - 1) * TILE, TILE)] if tile < tiles else blank
            turned = jnp.dot(
                jnp.concatenate([lower, upper], axis=1), mirror, preferred_element_type=jnp.float32
            )
            width = TILE if tile < tiles else LANES
            flip_ref[:, pl.ds(LANES + tile * TILE, width)] = turned[:, :width]

    columns = pltpu.roll(code_ref[...], lax.rem(LANES - step_id * GROUP, LANES), 1)
    at_lane = lax.broadcasted_iota(jnp.int32, (partner_count, dest_rows), 1).astype(jnp.float32)
    chosen = jnp.concatenate(
        [
            (at_lane == columns[:, member : member + 1]).astype(jnp.bfloat16)
            for member in range(GROUP)
        ],
        axis=0,
    )
    picked = jnp.dot(chosen, bank_ref[:dest_rows, :], preferred_element_type=jnp.float32)
    picked_ref[...] = picked[:, :time_total].astype(jnp.bfloat16)
    partner_scale = picked[:, time_total : time_total + LANES] + picked[:, time_total + LANES :]
    blank = jnp.zeros((LANES, LANES), jnp.bfloat16)
    window_scale = 1.0 / (float(time_total) ** 0.5)
    first_row = step_id * GROUP
    for member in range(GROUP):
        row = flip_ref[pl.ds(first_row + member, 1), :]
        wide = shifted_rows(row.astype(jnp.bfloat16), LANES)

        def diagonal(k):
            if k < 0 or k > time_total // LANES:
                return blank
            start = time_total + LANES - LANES * k
            return wide[:, start : start + LANES]

        def band(first, last):
            return jnp.concatenate(
                [
                    jnp.concatenate([diagonal(k), diagonal(k - 1)], axis=1)
                    for k in range(2 * first, 2 * last)
                ],
                axis=0,
            )

        part = slice(member * partner_count, (member + 1) * partner_count)
        rows = picked_ref[part, :]
        inner = time_total - TILE
        both = jnp.dot(
            jnp.concatenate([rows[:, :inner], rows[:, TILE:]], axis=0),
            band(1, tiles),
            preferred_element_type=jnp.float32,
        )
        before = both[:partner_count] + jnp.dot(
            rows[:, inner:], band(tiles, tiles + 1), preferred_element_type=jnp.float32
        )
        after = both[partner_count:] + jnp.dot(
            rows[:, :TILE], band(0, 1), preferred_element_type=jnp.float32
        )
        scale = partner_scale[part] * scale_ref[pl.ds(first_row + member, 1), :] * window_scale
        scale = jnp.concatenate([scale, scale], axis=1)
        out_ref[0, member, :, :TILE] = (before * scale).astype(jnp.bfloat16)
        out_ref[0, member, :, TILE:] = (after * scale).astype(jnp.bfloat16)


def per_device(raw_strain, spatial_filter, temporal_filter, dest_blocks, partner_codes):
    taps_here, time_step = raw_strain.shape
    lag_devices = lax.axis_size("lag")
    time_devices = lax.axis_size("tm")
    time_total = time_step * time_devices
    block_taps = taps_here // lag_devices
    dest_count = dest_blocks.shape[1]
    _, source_count, partner_count = partner_codes.shape
    cables = gathered(raw_strain)
    rows_all = dest_count * block_taps + source_count
    wide = time_total + 2 * LANES
    body = functools.partial(
        correlate_body,
        cable_count=len(cables),
        lag_devices=lag_devices,
        time_devices=time_devices,
    )
    return pl.pallas_call(
        body,
        grid_spec=pltpu.PrefetchScalarGridSpec(
            num_scalar_prefetch=1,
            grid=(source_count // GROUP,),
            in_specs=[
                pl.BlockSpec(partner_codes.shape, lambda i, t: (0, 0, 0)),
                pl.BlockSpec(spatial_filter.shape, lambda i, t: (0,)),
                pl.BlockSpec(temporal_filter.shape, lambda i, t: (0,)),
            ]
            + [pl.BlockSpec(memory_space=pl.ANY)] * len(cables),
            out_specs=pl.BlockSpec((1, GROUP, partner_count, LAG_COUNT), lambda i, t: (0, i, 0, 0)),
            scratch_shapes=[
                pltpu.VMEM((dest_count + 1, block_taps + 2 * HALO, time_total), jnp.bfloat16),
                pltpu.VMEM((rows_all, wide), jnp.bfloat16),
                pltpu.VMEM((rows_all, wide), jnp.bfloat16),
                pltpu.VMEM((source_count, wide), jnp.float32),
                pltpu.VMEM((source_count, LANES), jnp.float32),
                pltpu.VMEM((partner_count, LANES), jnp.float32),
                pltpu.VMEM((GROUP * partner_count, time_total), jnp.bfloat16),
                pltpu.SemaphoreType.DMA((dest_count + 1, 3 * time_devices)),
            ],
        ),
        out_shape=jax.ShapeDtypeStruct((1, source_count, partner_count, LAG_COUNT), jnp.bfloat16),
        compiler_params=pltpu.CompilerParams(vmem_limit_bytes=56 << 20),
    )(dest_blocks, partner_codes, spatial_filter, temporal_filter, *cables)


def solution(mesh):
    placed = (
        P(("groups", "tap"), "tm"),
        P(),
        P(),
        P("groups", None),
        P(("groups", "tap", "lag"), "tm", None),
    )
    return jax.shard_map(
        per_device,
        mesh=mesh,
        in_specs=placed,
        out_specs=P(("groups", "tap", "lag"), "tm", None, None),
        check_vma=False,
    )
```

time: 51.3 us -> 44.6 us (0.87)
  other arithmetic: 3.47 us -> 0.14 us
  waiting for transfers between devices: 15.9 us -> 13.1 us
    ppermute x8 -> x9, waiting for transfers between devices: 15.9 us -> 13.1 us  [shifted(): lax.ppermute(cells, axis, [(i, (i + step) % count) for i in range(count)])]
    unnamed x10 -> x11, local copies, waits for them, and re-layouts: 1.22 us -> 3.47 us
    convert_element_type x1 -> x0, other arithmetic: 1.69 us -> none  [per_device(): (codes == jnp.arange(dest_rows, dtype=jnp.int32)[None, :]).astype(jnp.bfl...]
    another operation x6 -> x2, other arithmetic: 1.78 us -> 0.14 us  [the longest x1 0.07 us: gathered(): mine = [jnp.stack(taps)]]
    pad x2 -> x0, local copies, waits for them, and re-layouts: 1.26 us -> none  [the longest x1 0.66 us: per_device(): jnp.pad(temporal_filter, (1, 2 * TILE - 1 - temporal_filter.shape[0]))]
    concatenate x1 -> x0, local copies, waits for them, and re-layouts: 0.67 us -> none  [per_device(): jnp.concatenate([lax.dynamic_index_in_dim(dest_blocks, block_here, 0, kee...]
    ppermute x8 -> x9, starting transfers between devices: 11 us -> 11.3 us  [shifted(): lax.ppermute(cells, axis, [(i, (i + step) % count) for i in range(count)])]
  transfers between devices with their start and end apart: 8 -> 9, of which waited for: 2 -> 5; matrix products, arithmetic and copies ran while one was open for 8% -> 3% of each run, Pallas kernels for 0% -> 0%
where the time goes in v2:
time: 44.6 us; the launch traced here: 44.3 us
  Pallas kernels  16.3 us (37%)
  waiting for transfers between devices  13.1 us (29%)
  starting transfers between devices  11.3 us (25%)
  local copies, waits for them, and re-layouts  3.49 us (8%)
    pallas_call x1, Pallas kernels, per_device(): pl.pallas_call(body, grid_spec=pltpu.PrefetchScalarGridSpec(num_scalar_pr...  16.3 us
    ppermute x9, waiting for transfers between devices, shifted(): lax.ppermute(cells, axis, [(i, (i + step) % count) for i in range(count)])  13.1 us
    ppermute x9, starting transfers between devices, shifted(): lax.ppermute(cells, axis, [(i, (i + step) % count) for i in range(count)])  11.3 us
    unnamed x11, local copies, waits for them, and re-layouts  3.47 us
  transfers between devices with their start and end apart: 9, of which 5 were waited for; matrix products, arithmetic and copies ran while one was open for 3% of the time, Pallas kernels for 0%

profile of v2, /device:TPU:0, one launch (start us, length us, event | category | flops | bytes accessed | tf_op | source)
XLA Modules:
  0.0 44.3 jit_solution(10695612472630973304)
XLA Ops:
  0.0 0.0 copy-start
  0.0 0.9 %copy-done = bf16[256,512]{1,0:T(8,128)(2,1)S(1)} copy-done((bf16[256,512]{1,0:T(8,128)(2,1)S(1)}, bf16[256,512]{1,0:T(8,128)(2,1)}, u32[]{:S(2)}) %copy-start) | copy-done | bytes 262168
  1.0 5.1 %collective-permute-start.2 = (bf16[128,512]{1,0:T(8,128)(2,1)S(1)}, bf16[128,512]{1,0:T(8,128)(2,1)S(1)}, u32[]{:S(2)}, u32[]{:S(2)}) collective-permute-start(bf16[128,512]{1,0:T(8,128)(2,1)S(1)} %constant_dynamic-slice_fusion), channel_id=1, source_target_pairs={{0,12},{4,0},{8,4},{12,8},{1,13},{5,1},{9,5},{13,9},{2,14},{6,2},{... | collective-permute-start | bytes 393224 | tf_op jit(solution)/shard_map/ppermute | solution.py:36
  6.1 0.0 collective-permute-start.1
  6.1 1.0 %collective-permute-start = (bf16[128,512]{1,0:T(8,128)(2,1)S(1)}, bf16[128,512]{1,0:T(8,128)(2,1)S(1)}, u32[]{:S(2)}, u32[]{:S(2)}) collective-permute-start(bf16[128,512]{1,0:T(8,128)(2,1)S(1)} %constant_dynamic-slice_fusion), channel_id=1, source_target_pairs={{0,4},{4,8},{8,12},{12,0},{1,5},{5,9},{9,13},{13,1},{2,6},{6,10},{... | collective-permute-start | bytes 393224 | tf_op jit(solution)/shard_map/ppermute | solution.py:36
  7.1 1.5 %collective-permute-start.3 = (bf16[128,512]{1,0:T(8,128)(2,1)S(1)}, bf16[128,512]{1,0:T(8,128)(2,1)S(1)}, u32[]{:S(2)}, u32[]{:S(2)}) collective-permute-start(bf16[128,512]{1,0:T(8,128)(2,1)S(1)} %constant_dynamic-slice_fusion), channel_id=1, source_target_pairs={{0,2},{2,0},{1,3},{3,1},{4,6},{6,4},{5,7},{7,5},{8,10},{10,8},{9,1... | collective-permute-start | bytes 393224 | tf_op jit(solution)/shard_map/ppermute | solution.py:36
  8.6 1.4 %collective-permute-done.2 = bf16[128,512]{1,0:T(8,128)(2,1)S(1)} collective-permute-done((bf16[128,512]{1,0:T(8,128)(2,1)S(1)}, bf16[128,512]{1,0:T(8,128)(2,1)S(1)}, u32[]{:S(2)}, u32[]{:S(2)}) %collective-permute-start.2) | collective-permute-done | bytes 131104 | tf_op jit(solution)/shard_map/ppermute | solution.py:36
  10.0 1.5 %collective-permute-start.6 = (bf16[128,512]{1,0:T(8,128)(2,1)S(1)}, bf16[128,512]{1,0:T(8,128)(2,1)S(1)}, u32[]{:S(2)}, u32[]{:S(2)}) collective-permute-start(bf16[128,512]{1,0:T(8,128)(2,1)S(1)} %collective-permute-done.2), channel_id=1, source_target_pairs={{0,2},{2,0},{1,3},{3,1},{4,6},{6,4},{5,7},{7,5},{8,10},{10,8},{9,1... | collective-permute-start | bytes 393224 | tf_op jit(solution)/shard_map/ppermute | solution.py:36
  11.5 5.8 %collective-permute-done.1 = bf16[128,512]{1,0:T(8,128)(2,1)S(1)} collective-permute-done((bf16[128,512]{1,0:T(8,128)(2,1)S(1)}, bf16[128,512]{1,0:T(8,128)(2,1)S(1)}, u32[]{:S(2)}, u32[]{:S(2)}) %collective-permute-start.1) | collective-permute-done | bytes 131104 | tf_op jit(solution)/shard_map/ppermute | solution.py:36
  17.3 1.5 %collective-permute-start.5 = (bf16[128,512]{1,0:T(8,128)(2,1)S(1)}, bf16[128,512]{1,0:T(8,128)(2,1)S(1)}, u32[]{:S(2)}, u32[]{:S(2)}) collective-permute-start(bf16[128,512]{1,0:T(8,128)(2,1)S(1)} %collective-permute-done.1), channel_id=1, source_target_pairs={{0,2},{2,0},{1,3},{3,1},{4,6},{6,4},{5,7},{7,5},{8,10},{10,8},{9,1... | collective-permute-start | bytes 393224 | tf_op jit(solution)/shard_map/ppermute | solution.py:36
  18.8 0.0 collective-permute-done
  18.8 0.5 %collective-permute-start.4 = (bf16[128,512]{1,0:T(8,128)(2,1)S(1)}, bf16[128,512]{1,0:T(8,128)(2,1)S(1)}, u32[]{:S(2)}, u32[]{:S(2)}) collective-permute-start(bf16[128,512]{1,0:T(8,128)(2,1)S(1)} %collective-permute-done), channel_id=1, source_target_pairs={{0,2},{2,0},{1,3},{3,1},{4,6},{6,4},{5,7},{7,5},{8,10},{10,8},{9,1... | collective-permute-start | bytes 393224 | tf_op jit(solution)/shard_map/ppermute | solution.py:36
  19.3 0.1 pad_maximum_fusion.refs_4_
  19.4 0.0 copy-start.1
  19.4 0.1 collective-permute-start.7
  19.5 0.0 collective-permute-done.3
  19.5 0.0 collective-permute-done.6
  19.5 3.9 %collective-permute-done.5 = bf16[128,512]{1,0:T(8,128)(2,1)S(1)} collective-permute-done((bf16[128,512]{1,0:T(8,128)(2,1)S(1)}, bf16[128,512]{1,0:T(8,128)(2,1)S(1)}, u32[]{:S(2)}, u32[]{:S(2)}) %collective-permute-start.5) | collective-permute-done | bytes 131104 | tf_op jit(solution)/shard_map/ppermute | solution.py:36
  23.4 1.4 %collective-permute-done.4 = bf16[128,512]{1,0:T(8,128)(2,1)S(1)} collective-permute-done((bf16[128,512]{1,0:T(8,128)(2,1)S(1)}, bf16[128,512]{1,0:T(8,128)(2,1)S(1)}, u32[]{:S(2)}, u32[]{:S(2)}) %collective-permute-start.4) | collective-permute-done | bytes 131104 | tf_op jit(solution)/shard_map/ppermute | solution.py:36
  24.8 0.1 pad_maximum_fusion.1.refs_5_
  24.9 0.0 copy-start.2
  24.9 0.1 collective-permute-start.8
  25.0 1.4 %copy.6.refs_0_ = s32[8,2]{1,0:T(8,128)} copy(s32[8,2]{0,1:T(2,128)} %param.8) | data formatting | bytes 128 | tf_op args[3]
  26.4 0.0 collective-permute-done.7.refs_6_
  26.4 0.0 copy-start.3
  26.4 0.5 %collective-permute-done.8.refs_7_ = bf16[4,128,512]{2,1,0:T(8,128)(2,1)S(1)} collective-permute-done((bf16[4,128,512]{2,1,0:T(8,128)(2,1)S(1)}, bf16[4,128,512]{2,1,0:T(8,128)(2,1)S(1)}, u32[]{:S(2)}, u32[]{:S(2)}) %collective-permute-start.8) | collective-permute-done | bytes 524320 | tf_op jit(solution)/shard_map/ppermute | solution.py:36
  26.9 0.0 copy-done.1
  26.9 0.0 copy-done.2
  26.9 0.3 copy-done.3
  27.2 0.0 copy-start.4
  27.2 0.8 %copy-done.4 = bf16[4,128,512]{2,1,0:T(8,128)(2,1)} copy-done((bf16[4,128,512]{2,1,0:T(8,128)(2,1)}, bf16[4,128,512]{2,1,0:T(8,128)(2,1)S(1)}, u32[]{:S(2)}) %copy-start.4) | copy-done | bytes 524312
  28.0 16.3 %shard_map.55 = bf16[1,64,64,512]{3,2,1,0:T(8,128)(2,1)} custom-call(s32[8,2]{1,0:T(8,128)} %copy.6.refs_0_, s32[1,64,64]{2,1,0:T(8,128)} %refs_1_.1, f32[33]{0:T(128)} %refs_2_.1, f32[255]{0:T(256)} %refs_3_.1, bf16[4,128,512]{2,1,0:T(8,128)(2,1)} %copy-done.1, bf16[4,128,512]{2,1,0:T(8,128)(2,1)} %copy-done.2, bf16[4,128,512]{2,1,0:T(8,128)(2,1)} %copy-done.3, ...), custom_call_target="tpu_custom_call" | custom-call | tf_op jit(solution)/shard_map/pallas_call | solution.py:241
  (2 shorter events, 0.0 us)
Async XLA Ops:
  0.0 1.0 %copy-start = (bf16[256,512]{1,0:T(8,128)(2,1)S(1)}, bf16[256,512]{1,0:T(8,128)(2,1)}, u32[]{:S(2)}) copy-start(bf16[256,512]{1,0:T(8,128)(2,1)} %param.5) | copy-start | bytes 786436
  1.0 9.0 %collective-permute-start.2 = (bf16[128,512]{1,0:T(8,128)(2,1)S(1)}, bf16[128,512]{1,0:T(8,128)(2,1)S(1)}, u32[]{:S(2)}, u32[]{:S(2)}) collective-permute-start(bf16[128,512]{1,0:T(8,128)(2,1)S(1)} %constant_dynamic-slice_fusion), channel_id=1, source_target_pairs={{0,12},{4,0},{8,4},{12,8},{1,13},{5,1},{9,5},{13,9},{2,14},{6,2},{... | collective-permute-start | bytes 393224 | tf_op jit(solution)/shard_map/ppermute | solution.py:36
  6.1 11.2 %collective-permute-start.1 = (bf16[128,512]{1,0:T(8,128)(2,1)S(1)}, bf16[128,512]{1,0:T(8,128)(2,1)S(1)}, u32[]{:S(2)}, u32[]{:S(2)}) collective-permute-start(bf16[128,512]{1,0:T(8,128)(2,1)S(1)} %constant_dynamic-slice_fusion), channel_id=1, source_target_pairs={{0,8},{4,12},{8,0},{12,4},{1,9},{5,13},{9,1},{13,5},{2,10},{6,14},... | collective-permute-start | bytes 393224 | tf_op jit(solution)/shard_map/ppermute | solution.py:36
  6.1 12.7 %collective-permute-start = (bf16[128,512]{1,0:T(8,128)(2,1)S(1)}, bf16[128,512]{1,0:T(8,128)(2,1)S(1)}, u32[]{:S(2)}, u32[]{:S(2)}) collective-permute-start(bf16[128,512]{1,0:T(8,128)(2,1)S(1)} %constant_dynamic-slice_fusion), channel_id=1, source_target_pairs={{0,4},{4,8},{8,12},{12,0},{1,5},{5,9},{9,13},{13,1},{2,6},{6,10},{... | collective-permute-start | bytes 393224 | tf_op jit(solution)/shard_map/ppermute | solution.py:36
  7.1 12.4 %collective-permute-start.3 = (bf16[128,512]{1,0:T(8,128)(2,1)S(1)}, bf16[128,512]{1,0:T(8,128)(2,1)S(1)}, u32[]{:S(2)}, u32[]{:S(2)}) collective-permute-start(bf16[128,512]{1,0:T(8,128)(2,1)S(1)} %constant_dynamic-slice_fusion), channel_id=1, source_target_pairs={{0,2},{2,0},{1,3},{3,1},{4,6},{6,4},{5,7},{7,5},{8,10},{10,8},{9,1... | collective-permute-start | bytes 393224 | tf_op jit(solution)/shard_map/ppermute | solution.py:36
  10.0 9.5 %collective-permute-start.6 = (bf16[128,512]{1,0:T(8,128)(2,1)S(1)}, bf16[128,512]{1,0:T(8,128)(2,1)S(1)}, u32[]{:S(2)}, u32[]{:S(2)}) collective-permute-start(bf16[128,512]{1,0:T(8,128)(2,1)S(1)} %collective-permute-done.2), channel_id=1, source_target_pairs={{0,2},{2,0},{1,3},{3,1},{4,6},{6,4},{5,7},{7,5},{8,10},{10,8},{9,1... | collective-permute-start | bytes 393224 | tf_op jit(solution)/shard_map/ppermute | solution.py:36
  17.3 6.2 %collective-permute-start.5 = (bf16[128,512]{1,0:T(8,128)(2,1)S(1)}, bf16[128,512]{1,0:T(8,128)(2,1)S(1)}, u32[]{:S(2)}, u32[]{:S(2)}) collective-permute-start(bf16[128,512]{1,0:T(8,128)(2,1)S(1)} %collective-permute-done.1), channel_id=1, source_target_pairs={{0,2},{2,0},{1,3},{3,1},{4,6},{6,4},{5,7},{7,5},{8,10},{10,8},{9,1... | collective-permute-start | bytes 393224 | tf_op jit(solution)/shard_map/ppermute | solution.py:36
  18.8 6.1 %collective-permute-start.4 = (bf16[128,512]{1,0:T(8,128)(2,1)S(1)}, bf16[128,512]{1,0:T(8,128)(2,1)S(1)}, u32[]{:S(2)}, u32[]{:S(2)}) collective-permute-start(bf16[128,512]{1,0:T(8,128)(2,1)S(1)} %collective-permute-done), channel_id=1, source_target_pairs={{0,2},{2,0},{1,3},{3,1},{4,6},{6,4},{5,7},{7,5},{8,10},{10,8},{9,1... | collective-permute-start | bytes 393224 | tf_op jit(solution)/shard_map/ppermute | solution.py:36
  19.4 7.5 %copy-start.1 = (bf16[4,128,512]{2,1,0:T(8,128)(2,1)}, bf16[4,128,512]{2,1,0:T(8,128)(2,1)S(1)}, u32[]{:S(2)}) copy-start(bf16[4,128,512]{2,1,0:T(8,128)(2,1)S(1)} %pad_maximum_fusion.refs_4_) | copy-start | bytes 1572868
  19.4 7.0 %collective-permute-start.7 = (bf16[4,128,512]{2,1,0:T(8,128)(2,1)S(1)}, bf16[4,128,512]{2,1,0:T(8,128)(2,1)S(1)}, u32[]{:S(2)}, u32[]{:S(2)}) collective-permute-start(bf16[4,128,512]{2,1,0:T(8,128)(2,1)S(1)} %pad_maximum_fusion.refs_4_), channel_id=1, source_target_pairs={{0,1},{1,0},{2,3},{3,2},{4,5},{5,4},{6,7},{7,6},{8,9},{9,8},{10,11... | collective-permute-start | bytes 1572872 | tf_op jit(solution)/shard_map/ppermute | solution.py:36
  24.9 2.0 %copy-start.2 = (bf16[4,128,512]{2,1,0:T(8,128)(2,1)}, bf16[4,128,512]{2,1,0:T(8,128)(2,1)S(1)}, u32[]{:S(2)}) copy-start(bf16[4,128,512]{2,1,0:T(8,128)(2,1)S(1)} %pad_maximum_fusion.1.refs_5_) | copy-start | bytes 1572868
  24.9 2.0 %collective-permute-start.8 = (bf16[4,128,512]{2,1,0:T(8,128)(2,1)S(1)}, bf16[4,128,512]{2,1,0:T(8,128)(2,1)S(1)}, u32[]{:S(2)}, u32[]{:S(2)}) collective-permute-start(bf16[4,128,512]{2,1,0:T(8,128)(2,1)S(1)} %pad_maximum_fusion.1.refs_5_), channel_id=1, source_target_pairs={{0,1},{1,0},{2,3},{3,2},{4,5},{5,4},{6,7},{7,6},{8,9},{9,8},{10,11... | collective-permute-start | bytes 1572872 | tf_op jit(solution)/shard_map/ppermute | solution.py:36
  26.4 0.8 %copy-start.3 = (bf16[4,128,512]{2,1,0:T(8,128)(2,1)}, bf16[4,128,512]{2,1,0:T(8,128)(2,1)S(1)}, u32[]{:S(2)}) copy-start(bf16[4,128,512]{2,1,0:T(8,128)(2,1)S(1)} %collective-permute-done.7.refs_6_) | copy-start | bytes 1572868
  27.2 0.8 %copy-start.4 = (bf16[4,128,512]{2,1,0:T(8,128)(2,1)}, bf16[4,128,512]{2,1,0:T(8,128)(2,1)S(1)}, u32[]{:S(2)}) copy-start(bf16[4,128,512]{2,1,0:T(8,128)(2,1)S(1)} %collective-permute-done.8.refs_7_) | copy-start | bytes 1572868

commit v3 on v2

--- a/solution.py
+++ b/solution.py
@@ -13,6 +13,7 @@
 TILE = 256
 LANES = 128
 GROUP = 16
+NEAR_CELLS = 2 << 20
 
 
 def split_parts(matrix):
@@ -35,7 +36,14 @@
         count = lax.axis_size(axis)
         return lax.ppermute(cells, axis, [(i, (i + step) % count) for i in range(count)])
 
-    taps = [half] + [shifted(half, "tap", step) for step in range(1, lax.axis_size("tap"))]
+    tap_devices = lax.axis_size("tap")
+    taps = [half]
+    for step in range(1, tap_devices // 2 + 1):
+        taps.append(shifted(taps[-1], "tap", 1))
+    behind = [half]
+    for step in range(1, (tap_devices + 1) // 2):
+        behind.append(shifted(behind[-1], "tap", tap_devices - 1))
+    taps += behind[:0:-1]
     mine = [jnp.stack(taps)]
     for step in range(1, lax.axis_size("tm")):
         mine.append(jnp.stack([shifted(cells, "tm", step) for cells in taps]))
@@ -53,7 +61,7 @@
     ]
     tap_devices, block_taps, time_step = cable_refs[0].shape
     _, source_count, partner_count = codes_ref.shape
-    dest_count = dest_ref.shape[1]
+    dest_count = dest_ref.shape[0]
     dest_rows = dest_count * block_taps
     time_total = time_devices * time_step
     tiles = time_total // TILE
@@ -100,7 +108,7 @@
 
     @pl.when(step_id == 0)
     def prepare():
-        blocks = [dest_ref[block_here, j] for j in range(dest_count)] + [block_here]
+        blocks = [dest_ref[j, block_here] for j in range(dest_count)] + [block_here]
         for segment, block in enumerate(blocks):
             start_all(segment, block)
         code_ref[:, :source_count] = codes_ref[0].astype(jnp.float32).T
@@ -230,6 +238,9 @@
     dest_count = dest_blocks.shape[1]
     _, source_count, partner_count = partner_codes.shape
     cables = gathered(raw_strain)
+    near = sum(cells.size for cells in cables) <= NEAR_CELLS
+    if near:
+        cables = [pltpu.with_memory_space_constraint(cells, pltpu.VMEM) for cells in cables]
     rows_all = dest_count * block_taps + source_count
     wide = time_total + 2 * LANES
     body = functools.partial(
@@ -248,7 +259,7 @@
                 pl.BlockSpec(spatial_filter.shape, lambda i, t: (0,)),
                 pl.BlockSpec(temporal_filter.shape, lambda i, t: (0,)),
             ]
-            + [pl.BlockSpec(memory_space=pl.ANY)] * len(cables),
+            + [pl.BlockSpec(memory_space=pltpu.VMEM if near else pl.ANY)] * len(cables),
             out_specs=pl.BlockSpec((1, GROUP, partner_count, LAG_COUNT), lambda i, t: (0, i, 0, 0)),
             scratch_shapes=[
                 pltpu.VMEM((dest_count + 1, block_taps + 2 * HALO, time_total), jnp.bfloat16),
@@ -263,7 +274,7 @@
         ),
         out_shape=jax.ShapeDtypeStruct((1, source_count, partner_count, LAG_COUNT), jnp.bfloat16),
         compiler_params=pltpu.CompilerParams(vmem_limit_bytes=56 << 20),
-    )(dest_blocks, partner_codes, spatial_filter, temporal_filter, *cables)
+    )(dest_blocks.T, partner_codes, spatial_filter, temporal_filter, *cables)
 
 
 def solution(mesh):

time: 44.6 us -> 40.9 us (0.917)
  local copies, waits for them, and re-layouts: 3.49 us -> 0.97 us
  starting transfers between devices: 11.3 us -> 10.8 us
    unnamed x11 -> x2, local copies, waits for them, and re-layouts: 3.47 us -> 0.95 us
    ppermute x9, starting transfers between devices: 11.3 us -> 10.8 us  [shifted(): lax.ppermute(cells, axis, [(i, (i + step) % count) for i in range(count)])]
  transfers between devices with their start and end apart: 9 -> 9, of which waited for: 5 -> 5; matrix products, arithmetic and copies ran while one was open for 3% -> 0% of each run, Pallas kernels for 0% -> 0%
where the time goes in v3:
time: 40.9 us; the launch traced here: 40.7 us
  Pallas kernels  15.9 us (39%)
  waiting for transfers between devices  12.8 us (31%)
  starting transfers between devices  10.8 us (26%)
  local copies, waits for them, and re-layouts  0.97 us (2%)
    pallas_call x1, Pallas kernels, per_device(): pl.pallas_call(body, grid_spec=pltpu.PrefetchScalarGridSpec(num_scalar_pr...  15.9 us
    ppermute x9, waiting for transfers between devices, shifted(): lax.ppermute(cells, axis, [(i, (i + step) % count) for i in range(count)])  12.8 us
    ppermute x9, starting transfers between devices, shifted(): lax.ppermute(cells, axis, [(i, (i + step) % count) for i in range(count)])  10.8 us
    unnamed x2, local copies, waits for them, and re-layouts  0.95 us
  transfers between devices with their start and end apart: 9, of which 5 were waited for; matrix products, arithmetic and copies ran while one was open for 0% of the time, Pallas kernels for 0%

profile of v3, /device:TPU:0, one launch (start us, length us, event | category | flops | bytes accessed | tf_op | source)
XLA Modules:
  0.0 40.7 jit_solution(17611234140278977556)
XLA Ops:
  0.0 0.0 copy-start
  0.0 0.9 %copy-done = bf16[256,512]{1,0:T(8,128)(2,1)S(1)} copy-done((bf16[256,512]{1,0:T(8,128)(2,1)S(1)}, bf16[256,512]{1,0:T(8,128)(2,1)}, u32[]{:S(2)}) %copy-start) | copy-done | bytes 262168
  1.0 3.1 %collective-permute-start = (bf16[128,512]{1,0:T(8,128)(2,1)S(1)}, bf16[128,512]{1,0:T(8,128)(2,1)S(1)}, u32[]{:S(2)}, u32[]{:S(2)}) collective-permute-start(bf16[128,512]{1,0:T(8,128)(2,1)S(1)} %constant_dynamic-slice_fusion), channel_id=1, source_target_pairs={{0,4},{4,8},{8,12},{12,0},{1,5},{5,9},{9,13},{13,1},{2,6},{6,10},{... | collective-permute-start | bytes 393224 | tf_op jit(solution)/shard_map/ppermute | solution.py:37
  4.0 2.1 %collective-permute-start.2 = (bf16[128,512]{1,0:T(8,128)(2,1)S(1)}, bf16[128,512]{1,0:T(8,128)(2,1)S(1)}, u32[]{:S(2)}, u32[]{:S(2)}) collective-permute-start(bf16[128,512]{1,0:T(8,128)(2,1)S(1)} %constant_dynamic-slice_fusion), channel_id=1, source_target_pairs={{0,12},{4,0},{8,4},{12,8},{1,13},{5,1},{9,5},{13,9},{2,14},{6,2},{... | collective-permute-start | bytes 393224 | tf_op jit(solution)/shard_map/ppermute | solution.py:37
  6.1 4.3 %collective-permute-done = bf16[128,512]{1,0:T(8,128)(2,1)S(1)} collective-permute-done((bf16[128,512]{1,0:T(8,128)(2,1)S(1)}, bf16[128,512]{1,0:T(8,128)(2,1)S(1)}, u32[]{:S(2)}, u32[]{:S(2)}) %collective-permute-start) | collective-permute-done | bytes 131104 | tf_op jit(solution)/shard_map/ppermute | solution.py:37
  10.4 0.0 collective-permute-start.1
  10.4 1.7 %collective-permute-start.3 = (bf16[128,512]{1,0:T(8,128)(2,1)S(1)}, bf16[128,512]{1,0:T(8,128)(2,1)S(1)}, u32[]{:S(2)}, u32[]{:S(2)}) collective-permute-start(bf16[128,512]{1,0:T(8,128)(2,1)S(1)} %constant_dynamic-slice_fusion), channel_id=1, source_target_pairs={{0,2},{2,0},{1,3},{3,1},{4,6},{6,4},{5,7},{7,5},{8,10},{10,8},{9,1... | collective-permute-start | bytes 393224 | tf_op jit(solution)/shard_map/ppermute | solution.py:37
  12.1 0.3 collective-permute-start.4
  12.4 0.0 collective-permute-done.2
  12.4 1.7 %collective-permute-start.6 = (bf16[128,512]{1,0:T(8,128)(2,1)S(1)}, bf16[128,512]{1,0:T(8,128)(2,1)S(1)}, u32[]{:S(2)}, u32[]{:S(2)}) collective-permute-start(bf16[128,512]{1,0:T(8,128)(2,1)S(1)} %collective-permute-done.2), channel_id=1, source_target_pairs={{0,2},{2,0},{1,3},{3,1},{4,6},{6,4},{5,7},{7,5},{8,10},{10,8},{9,1... | collective-permute-start | bytes 393224 | tf_op jit(solution)/shard_map/ppermute | solution.py:37
  14.2 3.0 %collective-permute-done.1 = bf16[128,512]{1,0:T(8,128)(2,1)S(1)} collective-permute-done((bf16[128,512]{1,0:T(8,128)(2,1)S(1)}, bf16[128,512]{1,0:T(8,128)(2,1)S(1)}, u32[]{:S(2)}, u32[]{:S(2)}) %collective-permute-start.1) | collective-permute-done | bytes 131104 | tf_op jit(solution)/shard_map/ppermute | solution.py:37
  17.2 1.7 %collective-permute-start.5 = (bf16[128,512]{1,0:T(8,128)(2,1)S(1)}, bf16[128,512]{1,0:T(8,128)(2,1)S(1)}, u32[]{:S(2)}, u32[]{:S(2)}) collective-permute-start(bf16[128,512]{1,0:T(8,128)(2,1)S(1)} %collective-permute-done.1), channel_id=1, source_target_pairs={{0,2},{2,0},{1,3},{3,1},{4,6},{6,4},{5,7},{7,5},{8,10},{10,8},{9,1... | collective-permute-start | bytes 393224 | tf_op jit(solution)/shard_map/ppermute | solution.py:37
  18.9 0.1 pad_maximum_fusion.refs_4_
  19.0 0.1 collective-permute-start.7
  19.1 0.0 collective-permute-done.3
  19.1 2.2 %collective-permute-done.6 = bf16[128,512]{1,0:T(8,128)(2,1)S(1)} collective-permute-done((bf16[128,512]{1,0:T(8,128)(2,1)S(1)}, bf16[128,512]{1,0:T(8,128)(2,1)S(1)}, u32[]{:S(2)}, u32[]{:S(2)}) %collective-permute-start.6) | collective-permute-done | bytes 131104 | tf_op jit(solution)/shard_map/ppermute | solution.py:37
  21.3 0.0 collective-permute-done.4
  21.3 1.4 %collective-permute-done.5 = bf16[128,512]{1,0:T(8,128)(2,1)S(1)} collective-permute-done((bf16[128,512]{1,0:T(8,128)(2,1)S(1)}, bf16[128,512]{1,0:T(8,128)(2,1)S(1)}, u32[]{:S(2)}, u32[]{:S(2)}) %collective-permute-start.5) | collective-permute-done | bytes 131104 | tf_op jit(solution)/shard_map/ppermute | solution.py:37
  22.7 0.1 pad_maximum_fusion.1.refs_5_
  22.8 0.1 collective-permute-start.8
  22.8 0.0 collective-permute-done.7.refs_6_
  22.8 1.9 %collective-permute-done.8.refs_7_ = bf16[4,128,512]{2,1,0:T(8,128)(2,1)S(1)} collective-permute-done((bf16[4,128,512]{2,1,0:T(8,128)(2,1)S(1)}, bf16[4,128,512]{2,1,0:T(8,128)(2,1)S(1)}, u32[]{:S(2)}, u32[]{:S(2)}) %collective-permute-start.8) | collective-permute-done | bytes 524320 | tf_op jit(solution)/shard_map/ppermute | solution.py:37
  24.7 15.9 %shard_map.55 = bf16[1,64,64,512]{3,2,1,0:T(8,128)(2,1)} custom-call(s32[2,8]{1,0:T(2,128)} %bitcast.17, s32[1,64,64]{2,1,0:T(8,128)} %refs_1_.1, f32[33]{0:T(128)} %refs_2_.1, f32[255]{0:T(256)} %refs_3_.1, bf16[4,128,512]{2,1,0:T(8,128)(2,1)S(1)} %pad_maximum_fusion.refs_4_, bf16[4,128,512]{2,1,0:T(8,128)(2,1)S(1)} %pad_maximum_fusion.1.refs_5_, ...), custom_call_target="tpu_custom_call" | custom-call | tf_op jit(solution)/shard_map/pallas_call | solution.py:252
  (2 shorter events, 0.0 us)
Async XLA Ops:
  0.0 1.0 %copy-start = (bf16[256,512]{1,0:T(8,128)(2,1)S(1)}, bf16[256,512]{1,0:T(8,128)(2,1)}, u32[]{:S(2)}) copy-start(bf16[256,512]{1,0:T(8,128)(2,1)} %param.5) | copy-start | bytes 786436
  1.0 9.4 %collective-permute-start = (bf16[128,512]{1,0:T(8,128)(2,1)S(1)}, bf16[128,512]{1,0:T(8,128)(2,1)S(1)}, u32[]{:S(2)}, u32[]{:S(2)}) collective-permute-start(bf16[128,512]{1,0:T(8,128)(2,1)S(1)} %constant_dynamic-slice_fusion), channel_id=1, source_target_pairs={{0,4},{4,8},{8,12},{12,0},{1,5},{5,9},{9,13},{13,1},{2,6},{6,10},{... | collective-permute-start | bytes 393224 | tf_op jit(solution)/shard_map/ppermute | solution.py:37
  4.0 8.4 %collective-permute-start.2 = (bf16[128,512]{1,0:T(8,128)(2,1)S(1)}, bf16[128,512]{1,0:T(8,128)(2,1)S(1)}, u32[]{:S(2)}, u32[]{:S(2)}) collective-permute-start(bf16[128,512]{1,0:T(8,128)(2,1)S(1)} %constant_dynamic-slice_fusion), channel_id=1, source_target_pairs={{0,12},{4,0},{8,4},{12,8},{1,13},{5,1},{9,5},{13,9},{2,14},{6,2},{... | collective-permute-start | bytes 393224 | tf_op jit(solution)/shard_map/ppermute | solution.py:37
  10.4 6.8 %collective-permute-start.1 = (bf16[128,512]{1,0:T(8,128)(2,1)S(1)}, bf16[128,512]{1,0:T(8,128)(2,1)S(1)}, u32[]{:S(2)}, u32[]{:S(2)}) collective-permute-start(bf16[128,512]{1,0:T(8,128)(2,1)S(1)} %collective-permute-done), channel_id=1, source_target_pairs={{0,4},{4,8},{8,12},{12,0},{1,5},{5,9},{9,13},{13,1},{2,6},{6,10},{... | collective-permute-start | bytes 393224 | tf_op jit(solution)/shard_map/ppermute | solution.py:37
  10.4 8.7 %collective-permute-start.3 = (bf16[128,512]{1,0:T(8,128)(2,1)S(1)}, bf16[128,512]{1,0:T(8,128)(2,1)S(1)}, u32[]{:S(2)}, u32[]{:S(2)}) collective-permute-start(bf16[128,512]{1,0:T(8,128)(2,1)S(1)} %constant_dynamic-slice_fusion), channel_id=1, source_target_pairs={{0,2},{2,0},{1,3},{3,1},{4,6},{6,4},{5,7},{7,5},{8,10},{10,8},{9,1... | collective-permute-start | bytes 393224 | tf_op jit(solution)/shard_map/ppermute | solution.py:37
  12.1 9.1 %collective-permute-start.4 = (bf16[128,512]{1,0:T(8,128)(2,1)S(1)}, bf16[128,512]{1,0:T(8,128)(2,1)S(1)}, u32[]{:S(2)}, u32[]{:S(2)}) collective-permute-start(bf16[128,512]{1,0:T(8,128)(2,1)S(1)} %collective-permute-done), channel_id=1, source_target_pairs={{0,2},{2,0},{1,3},{3,1},{4,6},{6,4},{5,7},{7,5},{8,10},{10,8},{9,1... | collective-permute-start | bytes 393224 | tf_op jit(solution)/shard_map/ppermute | solution.py:37
  12.4 8.8 %collective-permute-start.6 = (bf16[128,512]{1,0:T(8,128)(2,1)S(1)}, bf16[128,512]{1,0:T(8,128)(2,1)S(1)}, u32[]{:S(2)}, u32[]{:S(2)}) collective-permute-start(bf16[128,512]{1,0:T(8,128)(2,1)S(1)} %collective-permute-done.2), channel_id=1, source_target_pairs={{0,2},{2,0},{1,3},{3,1},{4,6},{6,4},{5,7},{7,5},{8,10},{10,8},{9,1... | collective-permute-start | bytes 393224 | tf_op jit(solution)/shard_map/ppermute | solution.py:37
  17.2 5.5 %collective-permute-start.5 = (bf16[128,512]{1,0:T(8,128)(2,1)S(1)}, bf16[128,512]{1,0:T(8,128)(2,1)S(1)}, u32[]{:S(2)}, u32[]{:S(2)}) collective-permute-start(bf16[128,512]{1,0:T(8,128)(2,1)S(1)} %collective-permute-done.1), channel_id=1, source_target_pairs={{0,2},{2,0},{1,3},{3,1},{4,6},{6,4},{5,7},{7,5},{8,10},{10,8},{9,1... | collective-permute-start | bytes 393224 | tf_op jit(solution)/shard_map/ppermute | solution.py:37
  19.0 3.8 %collective-permute-start.7 = (bf16[4,128,512]{2,1,0:T(8,128)(2,1)S(1)}, bf16[4,128,512]{2,1,0:T(8,128)(2,1)S(1)}, u32[]{:S(2)}, u32[]{:S(2)}) collective-permute-start(bf16[4,128,512]{2,1,0:T(8,128)(2,1)S(1)} %pad_maximum_fusion.refs_4_), channel_id=1, source_target_pairs={{0,1},{1,0},{2,3},{3,2},{4,5},{5,4},{6,7},{7,6},{8,9},{9,8},{10,11... | collective-permute-start | bytes 1572872 | tf_op jit(solution)/shard_map/ppermute | solution.py:37
  22.8 2.0 %collective-permute-start.8 = (bf16[4,128,512]{2,1,0:T(8,128)(2,1)S(1)}, bf16[4,128,512]{2,1,0:T(8,128)(2,1)S(1)}, u32[]{:S(2)}, u32[]{:S(2)}) collective-permute-start(bf16[4,128,512]{2,1,0:T(8,128)(2,1)S(1)} %pad_maximum_fusion.1.refs_5_), channel_id=1, source_target_pairs={{0,1},{1,0},{2,3},{3,2},{4,5},{5,4},{6,7},{7,6},{8,9},{9,8},{10,11... | collective-permute-start | bytes 1572872 | tf_op jit(solution)/shard_map/ppermute | solution.py:37

commit v4 on v3

--- a/solution.py
+++ b/solution.py
@@ -27,7 +27,7 @@
     return pltpu.roll(wide, 0, 1, stride=1, stride_axis=0)
 
 
-def gathered(raw):
+def gathered(raw, bands):
     lag_devices = lax.axis_size("lag")
     half_rows = raw.shape[0] // lag_devices
     half = lax.dynamic_slice_in_dim(raw, lax.axis_index("lag") * half_rows, half_rows, 0)
@@ -37,30 +37,66 @@
         return lax.ppermute(cells, axis, [(i, (i + step) % count) for i in range(count)])
 
     tap_devices = lax.axis_size("tap")
-    taps = [half]
+    ahead, behind = [half], [half]
     for step in range(1, tap_devices // 2 + 1):
-        taps.append(shifted(taps[-1], "tap", 1))
-    behind = [half]
+        ahead.append(shifted(ahead[-1], "tap", 1))
+        if step == 1:
+            ahead[1], *bands = lax.optimization_barrier((ahead[1], *bands))
     for step in range(1, (tap_devices + 1) // 2):
         behind.append(shifted(behind[-1], "tap", tap_devices - 1))
-    taps += behind[:0:-1]
-    mine = [jnp.stack(taps)]
+    taps = ahead + behind[:0:-1]
+    mine = [None]
     for step in range(1, lax.axis_size("tm")):
-        mine.append(jnp.stack([shifted(cells, "tm", step) for cells in taps]))
+        swapped = shifted(half, "tm", step)
+        if step == 1 and tap_devices > 2:
+            taps[2], swapped = lax.optimization_barrier((taps[2], swapped))
+        mine.append(jnp.stack([swapped] + [shifted(cells, "tm", step) for cells in taps[1:]]))
+    mine[0] = jnp.stack(taps)
     cables = list(mine)
     for step in range(1, lag_devices):
         cables += [shifted(cells, "lag", step) for cells in mine]
-    return cables
-
-
-def correlate_body(*refs, cable_count, lag_devices, time_devices):
-    dest_ref, codes_ref, space_ref, time_ref = refs[:4]
+    return cables, bands
+
+
+def bands_body(dest_ref, codes_ref, space_ref, time_ref, space_out, time_out, code_out, *, block_total):
+    _, source_count, partner_count = codes_ref.shape
+    rows_all, ext_rows = space_out.shape[1:]
+    dest_count = dest_ref.shape[0]
+    block_taps = ext_rows - 2 * HALO
+    tap_index = lax.axis_index("tap")
+    time_index = lax.axis_index("tm")
+    block_here = tap_index * lax.axis_size("lag") + lax.axis_index("lag")
+    code_out[:, :source_count] = codes_ref[0].astype(jnp.float32).T
+    space_row = jnp.pad(space_ref[...][None, :], ((0, 0), (0, TILE - space_ref.shape[0])))
+    for segment in range(dest_count + 1):
+        own = segment == dest_count
+        block = block_here if own else dest_ref[segment, block_here]
+        row_count = source_count if own else block_taps
+        wide = shifted_rows(space_row, row_count)
+        if own:
+            wide = pltpu.roll(wide, time_index * source_count, 1)
+        rows_at = lax.broadcasted_iota(jnp.int32, (row_count, ext_rows), 1)
+        first = jnp.where(block == 0, HALO, 0)
+        last = jnp.where(block == block_total - 1, HALO + block_taps, ext_rows)
+        inside = jnp.logical_and(rows_at >= first, rows_at < last)
+        high, low = split_parts(jnp.where(inside, wide[:, :ext_rows], 0.0))
+        rows = slice(segment * block_taps, segment * block_taps + row_count)
+        space_out[0, rows, :] = high
+        space_out[1, rows, :] = low
+    time_row = jnp.pad(time_ref[...][None, :], ((0, 0), (1, 2 * TILE - 1 - time_ref.shape[0])))
+    high, low = split_parts(shifted_rows(time_row, TILE).T)
+    time_out[0] = high
+    time_out[1] = low
+
+
+def correlate_body(*refs, near, cable_count, lag_devices, time_devices):
+    dest_ref, space_ref, time_ref, code_ref = refs[:4]
     cable_refs = refs[4 : 4 + cable_count]
-    out_ref, raw_ref, smooth_ref, bank_ref, flip_ref, scale_ref, code_ref, picked_ref, sems = refs[
+    out_ref, raw_ref, smooth_ref, bank_ref, flip_ref, scale_ref, picked_ref, sems = refs[
         4 + cable_count :
     ]
     tap_devices, block_taps, time_step = cable_refs[0].shape
-    _, source_count, partner_count = codes_ref.shape
+    source_count, partner_count = flip_ref.shape[0], code_ref.shape[0]
     dest_count = dest_ref.shape[0]
     dest_rows = dest_count * block_taps
     time_total = time_devices * time_step
@@ -86,71 +122,57 @@
                 time_back = lax.rem(time_index - time_at + time_devices, time_devices)
                 cable_at = lag_step * time_devices + time_back
 
-                def copy_from(ref):
-                    return pltpu.make_async_copy(
+                def copy_from(
+                    ref, wait=False, tap_step=tap_step, part=part, time_at=time_at,
+                    source=source, target=target, size=size,
+                ):
+                    times = pl.ds(time_at * time_step, time_step)
+                    if near:
+                        raw_ref[segment, pl.ds(target, size), times] = ref[
+                            tap_step, pl.ds(source, size)
+                        ]
+                        return
+                    copy = pltpu.make_async_copy(
                         ref.at[tap_step, pl.ds(source, size)],
-                        raw_ref.at[
-                            segment, pl.ds(target, size), pl.ds(time_at * time_step, time_step)
-                        ],
+                        raw_ref.at[segment, pl.ds(target, size), times],
                         sems.at[segment, part * time_devices + time_at],
                     )
+                    copy.wait() if wait else copy.start()
 
                 yield cable_at, copy_from
 
     def start_all(segment, block):
         for cable_at, copy_from in pieces(segment, block):
             for i, ref in enumerate(cable_refs):
-                pl.when(cable_at == i)(lambda ref=ref, copy_from=copy_from: copy_from(ref).start())
+                pl.when(cable_at == i)(lambda ref=ref, copy_from=copy_from: copy_from(ref))
 
     def wait_all(segment, block):
-        for _, copy_from in pieces(segment, block):
-            copy_from(cable_refs[0]).wait()
+        if not near:
+            for _, copy_from in pieces(segment, block):
+                copy_from(cable_refs[0], wait=True)
 
     @pl.when(step_id == 0)
     def prepare():
         blocks = [dest_ref[j, block_here] for j in range(dest_count)] + [block_here]
         for segment, block in enumerate(blocks):
             start_all(segment, block)
-        code_ref[:, :source_count] = codes_ref[0].astype(jnp.float32).T
-        space_row = jnp.pad(space_ref[...][None, :], ((0, 0), (0, TILE - space_ref.shape[0])))
-        time_row = jnp.pad(time_ref[...][None, :], ((0, 0), (1, 2 * TILE - 1 - time_ref.shape[0])))
-        rows_at = lax.broadcasted_iota(jnp.int32, (block_taps, ext_rows), 1)
-        space_wide = shifted_rows(space_row, block_taps)[:, :ext_rows]
-        time_wide = shifted_rows(time_row, TILE)
-        time_high, time_low = split_parts(time_wide)
         smooth_ref[:, :LANES] = jnp.zeros((rows_all, LANES), jnp.bfloat16)
         smooth_ref[:, pl.ds(LANES + time_total, LANES)] = jnp.zeros((rows_all, LANES), jnp.bfloat16)
         for segment, block in enumerate(blocks):
             wait_all(segment, block)
-            first = jnp.where(block == 0, HALO, 0)
-            last = jnp.where(block == block_total - 1, HALO + block_taps, ext_rows)
-            inside = jnp.logical_and(rows_at >= first, rows_at < last)
-            space_high, space_low = split_parts(jnp.where(inside, space_wide, 0.0))
+            first = segment * block_taps
+            rows = slice(first, first + (block_taps if segment < dest_count else source_count))
             strain = raw_ref[segment]
-            smooth = jnp.dot(space_high, strain, preferred_element_type=jnp.float32)
-            smooth = smooth + jnp.dot(space_low, strain, preferred_element_type=jnp.float32)
-            smooth = smooth.astype(jnp.bfloat16)
-            if segment < dest_count:
-                smooth_ref[
-                    segment * block_taps : (segment + 1) * block_taps, pl.ds(LANES, time_total)
-                ] = smooth
-            else:
-                for part in range(time_devices):
-                    @pl.when(time_index == part)
-                    def keep_own():
-                        smooth_ref[dest_rows:, pl.ds(LANES, time_total)] = smooth[
-                            part * source_count : (part + 1) * source_count
-                        ]
-        transposed = (((1,), (1,)), ((), ()))
+            smooth = jnp.dot(space_ref[0, rows], strain, preferred_element_type=jnp.float32)
+            smooth = smooth + jnp.dot(
+                space_ref[1, rows], strain, preferred_element_type=jnp.float32
+            )
+            smooth_ref[rows, pl.ds(LANES, time_total)] = smooth.astype(jnp.bfloat16)
         power = jnp.zeros((rows_all, 1), jnp.float32)
         for tile in range(tiles):
             window = smooth_ref[:, tile * TILE : tile * TILE + 2 * TILE]
-            white = lax.dot_general(
-                window, time_high, transposed, preferred_element_type=jnp.float32
-            )
-            white = white + lax.dot_general(
-                window, time_low, transposed, preferred_element_type=jnp.float32
-            )
+            white = jnp.dot(window, time_ref[0], preferred_element_type=jnp.float32)
+            white = white + jnp.dot(window, time_ref[1], preferred_element_type=jnp.float32)
             white = white.astype(jnp.bfloat16)
             bank_ref[:, tile * TILE : (tile + 1) * TILE] = white
             white = white.astype(jnp.float32)
@@ -211,18 +233,16 @@
 
         part = slice(member * partner_count, (member + 1) * partner_count)
         rows = picked_ref[part, :]
-        inner = time_total - TILE
+        edge = jnp.zeros((partner_count, TILE), jnp.bfloat16)
         both = jnp.dot(
-            jnp.concatenate([rows[:, :inner], rows[:, TILE:]], axis=0),
-            band(1, tiles),
+            jnp.concatenate(
+                [jnp.concatenate([edge, rows], axis=1), jnp.concatenate([rows, edge], axis=1)],
+                axis=0,
+            ),
+            band(0, tiles + 1),
             preferred_element_type=jnp.float32,
         )
-        before = both[:partner_count] + jnp.dot(
-            rows[:, inner:], band(tiles, tiles + 1), preferred_element_type=jnp.float32
-        )
-        after = both[partner_count:] + jnp.dot(
-            rows[:, :TILE], band(0, 1), preferred_element_type=jnp.float32
-        )
+        before, after = both[:partner_count], both[partner_count:]
         scale = partner_scale[part] * scale_ref[pl.ds(first_row + member, 1), :] * window_scale
         scale = jnp.concatenate([scale, scale], axis=1)
         out_ref[0, member, :, :TILE] = (before * scale).astype(jnp.bfloat16)
@@ -237,14 +257,31 @@
     block_taps = taps_here // lag_devices
     dest_count = dest_blocks.shape[1]
     _, source_count, partner_count = partner_codes.shape
-    cables = gathered(raw_strain)
+    rows_all = dest_count * block_taps + source_count
+    placed = pl.BlockSpec(memory_space=pltpu.VMEM)
+    bands = pl.pallas_call(
+        functools.partial(bands_body, block_total=dest_blocks.shape[0]),
+        grid_spec=pltpu.PrefetchScalarGridSpec(
+            num_scalar_prefetch=1,
+            grid=(),
+            in_specs=[placed] * 3,
+            out_specs=[placed] * 3,
+        ),
+        out_shape=[
+            pltpu.VMEM((2, rows_all, block_taps + 2 * HALO), jnp.bfloat16),
+            pltpu.VMEM((2, 2 * TILE, TILE), jnp.bfloat16),
+            pltpu.VMEM((partner_count, LANES), jnp.float32),
+        ],
+    )(dest_blocks.T, partner_codes, spatial_filter, temporal_filter)
+    cables, bands = gathered(raw_strain, bands)
+    bands = [pltpu.with_memory_space_constraint(band, pltpu.VMEM) for band in bands]
     near = sum(cells.size for cells in cables) <= NEAR_CELLS
     if near:
         cables = [pltpu.with_memory_space_constraint(cells, pltpu.VMEM) for cells in cables]
-    rows_all = dest_count * block_taps + source_count
     wide = time_total + 2 * LANES
     body = functools.partial(
         correlate_body,
+        near=near,
         cable_count=len(cables),
         lag_devices=lag_devices,
         time_devices=time_devices,
@@ -254,12 +291,7 @@
         grid_spec=pltpu.PrefetchScalarGridSpec(
             num_scalar_prefetch=1,
             grid=(source_count // GROUP,),
-            in_specs=[
-                pl.BlockSpec(partner_codes.shape, lambda i, t: (0, 0, 0)),
-                pl.BlockSpec(spatial_filter.shape, lambda i, t: (0,)),
-                pl.BlockSpec(temporal_filter.shape, lambda i, t: (0,)),
-            ]
-            + [pl.BlockSpec(memory_space=pltpu.VMEM if near else pl.ANY)] * len(cables),
+            in_specs=[placed] * 3 + [placed if near else pl.BlockSpec(memory_space=pl.ANY)] * len(cables),
             out_specs=pl.BlockSpec((1, GROUP, partner_count, LAG_COUNT), lambda i, t: (0, i, 0, 0)),
             scratch_shapes=[
                 pltpu.VMEM((dest_count + 1, block_taps + 2 * HALO, time_total), jnp.bfloat16),
@@ -267,14 +299,13 @@
                 pltpu.VMEM((rows_all, wide), jnp.bfloat16),
                 pltpu.VMEM((source_count, wide), jnp.float32),
                 pltpu.VMEM((source_count, LANES), jnp.float32),
-                pltpu.VMEM((partner_count, LANES), jnp.float32),
                 pltpu.VMEM((GROUP * partner_count, time_total), jnp.bfloat16),
                 pltpu.SemaphoreType.DMA((dest_count + 1, 3 * time_devices)),
             ],
         ),
         out_shape=jax.ShapeDtypeStruct((1, source_count, partner_count, LAG_COUNT), jnp.bfloat16),
         compiler_params=pltpu.CompilerParams(vmem_limit_bytes=56 << 20),
-    )(dest_blocks.T, partner_codes, spatial_filter, temporal_filter, *cables)
+    )(dest_blocks.T, *bands, *cables)
 
 
 def solution(mesh):

time: 40.9 us -> 37.6 us (0.919)
  waiting for transfers between devices: 12.8 us -> 7.97 us
  starting transfers between devices: 10.8 us -> 13 us
  Pallas kernels: 15.9 us -> 15.2 us
    ppermute x9, waiting for transfers between devices: 12.8 us -> 7.97 us  [shifted(): lax.ppermute(cells, axis, [(i, (i + step) % count) for i in range(count)])]
    pallas_call x1, Pallas kernels: 15.9 us -> 13.5 us  [per_device(): pl.pallas_call(body, grid_spec=pltpu.PrefetchScalarGridSpec(num_scalar_pr...]
    ppermute x9, starting transfers between devices: 10.8 us -> 13 us  [shifted(): lax.ppermute(cells, axis, [(i, (i + step) % count) for i in range(count)])]
    pallas_call x0 -> x1, Pallas kernels: none -> 1.79 us  [per_device(): pl.pallas_call(functools.partial(bands_body, block_total=dest_blocks.shap...]
  transfers between devices with their start and end apart: 9 -> 9, of which waited for: 5 -> 5; matrix products, arithmetic and copies ran while one was open for 0% -> 0% of each run, Pallas kernels for 0% -> 5%
where the time goes in v4:
time: 37.6 us; the launch traced here: 37.3 us
  Pallas kernels  15.2 us (40%)
  starting transfers between devices  13 us (35%)
  waiting for transfers between devices  7.97 us (21%)
  local copies, waits for them, and re-layouts  0.97 us (3%)
    pallas_call x1, Pallas kernels, per_device(): pl.pallas_call(body, grid_spec=pltpu.PrefetchScalarGridSpec(num_scalar_pr...  13.5 us
    ppermute x9, starting transfers between devices, shifted(): lax.ppermute(cells, axis, [(i, (i + step) % count) for i in range(count)])  13 us
    ppermute x9, waiting for transfers between devices, shifted(): lax.ppermute(cells, axis, [(i, (i + step) % count) for i in range(count)])  7.97 us
    pallas_call x1, Pallas kernels, per_device(): pl.pallas_call(functools.partial(bands_body, block_total=dest_blocks.shap...  1.79 us
    unnamed x2, local copies, waits for them, and re-layouts  0.95 us
  transfers between devices with their start and end apart: 9, of which 5 were waited for; matrix products, arithmetic and copies ran while one was open for 0% of the time, Pallas kernels for 5%

profile of v4, /device:TPU:0, one launch (start us, length us, event | category | flops | bytes accessed | tf_op | source)
XLA Modules:
  0.0 37.3 jit_solution(5456747993382854238)
XLA Ops:
  0.0 0.0 copy-start
  0.0 0.9 %copy-done = bf16[256,512]{1,0:T(8,128)(2,1)S(1)} copy-done((bf16[256,512]{1,0:T(8,128)(2,1)S(1)}, bf16[256,512]{1,0:T(8,128)(2,1)}, u32[]{:S(2)}) %copy-start) | copy-done | bytes 262168
  1.0 3.1 %collective-permute-start = (bf16[128,512]{1,0:T(8,128)(2,1)S(1)}, bf16[128,512]{1,0:T(8,128)(2,1)S(1)}, u32[]{:S(2)}, u32[]{:S(2)}) collective-permute-start(bf16[128,512]{1,0:T(8,128)(2,1)S(1)} %constant_dynamic-slice_fusion), channel_id=1, source_target_pairs={{0,4},{4,8},{8,12},{12,0},{1,5},{5,9},{9,13},{13,1},{2,6},{6,10},{... | collective-permute-start | bytes 393224 | tf_op jit(solution)/shard_map/ppermute | solution.py:37
  4.0 1.5 %collective-permute-start.2 = (bf16[128,512]{1,0:T(8,128)(2,1)S(1)}, bf16[128,512]{1,0:T(8,128)(2,1)S(1)}, u32[]{:S(2)}, u32[]{:S(2)}) collective-permute-start(bf16[128,512]{1,0:T(8,128)(2,1)S(1)} %constant_dynamic-slice_fusion), channel_id=1, source_target_pairs={{0,2},{2,0},{1,3},{3,1},{4,6},{6,4},{5,7},{7,5},{8,10},{10,8},{9,1... | collective-permute-start | bytes 393224 | tf_op jit(solution)/shard_map/ppermute | solution.py:37
  5.5 2.2 %collective-permute-start.3 = (bf16[128,512]{1,0:T(8,128)(2,1)S(1)}, bf16[128,512]{1,0:T(8,128)(2,1)S(1)}, u32[]{:S(2)}, u32[]{:S(2)}) collective-permute-start(bf16[128,512]{1,0:T(8,128)(2,1)S(1)} %constant_dynamic-slice_fusion), channel_id=1, source_target_pairs={{0,12},{4,0},{8,4},{12,8},{1,13},{5,1},{9,5},{13,9},{2,14},{6,2},{... | collective-permute-start | bytes 393224 | tf_op jit(solution)/shard_map/ppermute | solution.py:37
  7.8 1.8 %shard_map.55 = (bf16[2,320,160]{2,1,0:T(8,128)(2,1)S(1)}, bf16[2,512,256]{2,1,0:T(8,128)(2,1)S(1)}, f32[64,128]{1,0:T(8,128)S(1)}) custom-call(s32[2,8]{1,0:T(2,128)} %bitcast.17, s32[1,64,64]{2,1,0:T(8,128)} %codes_ref.1, f32[33]{0:T(128)} %space_ref.1, f32[255]{0:T(256)} %time_ref.1), custom_call_target="tpu_custom_call" | custom-call | tf_op jit(solution)/shard_map/pallas_call | solution.py:262
  9.6 0.1 collective-permute-done
  9.7 0.0 collective-permute-start.1
  9.7 2.4 %collective-permute-start.4 = (bf16[128,512]{1,0:T(8,128)(2,1)S(1)}, bf16[128,512]{1,0:T(8,128)(2,1)S(1)}, u32[]{:S(2)}, u32[]{:S(2)}) collective-permute-start(bf16[128,512]{1,0:T(8,128)(2,1)S(1)} %collective-permute-done), channel_id=1, source_target_pairs={{0,2},{2,0},{1,3},{3,1},{4,6},{6,4},{5,7},{7,5},{8,10},{10,8},{9,1... | collective-permute-start | bytes 393224 | tf_op jit(solution)/shard_map/ppermute | solution.py:37
  12.1 0.2 collective-permute-done.3
  12.4 1.2 %collective-permute-start.6 = (bf16[128,512]{1,0:T(8,128)(2,1)S(1)}, bf16[128,512]{1,0:T(8,128)(2,1)S(1)}, u32[]{:S(2)}, u32[]{:S(2)}) collective-permute-start(bf16[128,512]{1,0:T(8,128)(2,1)S(1)} %collective-permute-done.3), channel_id=1, source_target_pairs={{0,2},{2,0},{1,3},{3,1},{4,6},{6,4},{5,7},{7,5},{8,10},{10,8},{9,1... | collective-permute-start | bytes 393224 | tf_op jit(solution)/shard_map/ppermute | solution.py:37
  13.6 0.0 collective-permute-done.2
  13.6 2.9 %collective-permute-done.1 = bf16[128,512]{1,0:T(8,128)(2,1)S(1)} collective-permute-done((bf16[128,512]{1,0:T(8,128)(2,1)S(1)}, bf16[128,512]{1,0:T(8,128)(2,1)S(1)}, u32[]{:S(2)}, u32[]{:S(2)}) %collective-permute-start.1) | collective-permute-done | bytes 131104 | tf_op jit(solution)/shard_map/ppermute | solution.py:37
  16.5 2.4 %collective-permute-start.5 = (bf16[128,512]{1,0:T(8,128)(2,1)S(1)}, bf16[128,512]{1,0:T(8,128)(2,1)S(1)}, u32[]{:S(2)}, u32[]{:S(2)}) collective-permute-start(bf16[128,512]{1,0:T(8,128)(2,1)S(1)} %collective-permute-done.1), channel_id=1, source_target_pairs={{0,2},{2,0},{1,3},{3,1},{4,6},{6,4},{5,7},{7,5},{8,10},{10,8},{9,1... | collective-permute-start | bytes 393224 | tf_op jit(solution)/shard_map/ppermute | solution.py:37
  18.9 0.1 pad_maximum_fusion.refs_4_
  19.0 0.1 collective-permute-start.7
  19.1 0.0 collective-permute-done.6
  19.1 0.0 collective-permute-done.4
  19.1 2.8 %collective-permute-done.5 = bf16[128,512]{1,0:T(8,128)(2,1)S(1)} collective-permute-done((bf16[128,512]{1,0:T(8,128)(2,1)S(1)}, bf16[128,512]{1,0:T(8,128)(2,1)S(1)}, u32[]{:S(2)}, u32[]{:S(2)}) %collective-permute-start.5) | collective-permute-done | bytes 131104 | tf_op jit(solution)/shard_map/ppermute | solution.py:37
  21.8 0.1 pad_maximum_fusion.1.refs_5_
  21.9 0.1 collective-permute-start.8
  22.0 0.0 collective-permute-done.7.refs_6_
  22.0 1.9 %collective-permute-done.8.refs_7_ = bf16[4,128,512]{2,1,0:T(8,128)(2,1)S(1)} collective-permute-done((bf16[4,128,512]{2,1,0:T(8,128)(2,1)S(1)}, bf16[4,128,512]{2,1,0:T(8,128)(2,1)S(1)}, u32[]{:S(2)}, u32[]{:S(2)}) %collective-permute-start.8) | collective-permute-done | bytes 524320 | tf_op jit(solution)/shard_map/ppermute | solution.py:37
  23.9 13.5 %shard_map.56 = bf16[1,64,64,512]{3,2,1,0:T(8,128)(2,1)} custom-call(s32[2,8]{1,0:T(2,128)} %bitcast.18, bf16[2,320,160]{2,1,0:T(8,128)(2,1)S(1)} %get-tuple-element.17.refs_1_, bf16[2,512,256]{2,1,0:T(8,128)(2,1)S(1)} %get-tuple-element.18.refs_2_, f32[64,128]{1,0:T(8,128)S(1)} %get-tuple-element.19.refs_3_, ...), custom_call_target="tpu_custom_call" | custom-call | tf_op jit(solution)/shard_map/pallas_call | solution.py:289
  (2 shorter events, 0.0 us)
Async XLA Ops:
  0.0 1.0 %copy-start = (bf16[256,512]{1,0:T(8,128)(2,1)S(1)}, bf16[256,512]{1,0:T(8,128)(2,1)}, u32[]{:S(2)}) copy-start(bf16[256,512]{1,0:T(8,128)(2,1)} %param.5) | copy-start | bytes 786436
  1.0 8.8 %collective-permute-start = (bf16[128,512]{1,0:T(8,128)(2,1)S(1)}, bf16[128,512]{1,0:T(8,128)(2,1)S(1)}, u32[]{:S(2)}, u32[]{:S(2)}) collective-permute-start(bf16[128,512]{1,0:T(8,128)(2,1)S(1)} %constant_dynamic-slice_fusion), channel_id=1, source_target_pairs={{0,4},{4,8},{8,12},{12,0},{1,5},{5,9},{9,13},{13,1},{2,6},{6,10},{... | collective-permute-start | bytes 393224 | tf_op jit(solution)/shard_map/ppermute | solution.py:37
  4.0 9.5 %collective-permute-start.2 = (bf16[128,512]{1,0:T(8,128)(2,1)S(1)}, bf16[128,512]{1,0:T(8,128)(2,1)S(1)}, u32[]{:S(2)}, u32[]{:S(2)}) collective-permute-start(bf16[128,512]{1,0:T(8,128)(2,1)S(1)} %constant_dynamic-slice_fusion), channel_id=1, source_target_pairs={{0,2},{2,0},{1,3},{3,1},{4,6},{6,4},{5,7},{7,5},{8,10},{10,8},{9,1... | collective-permute-start | bytes 393224 | tf_op jit(solution)/shard_map/ppermute | solution.py:37
  5.5 6.8 %collective-permute-start.3 = (bf16[128,512]{1,0:T(8,128)(2,1)S(1)}, bf16[128,512]{1,0:T(8,128)(2,1)S(1)}, u32[]{:S(2)}, u32[]{:S(2)}) collective-permute-start(bf16[128,512]{1,0:T(8,128)(2,1)S(1)} %constant_dynamic-slice_fusion), channel_id=1, source_target_pairs={{0,12},{4,0},{8,4},{12,8},{1,13},{5,1},{9,5},{13,9},{2,14},{6,2},{... | collective-permute-start | bytes 393224 | tf_op jit(solution)/shard_map/ppermute | solution.py:37
  9.7 6.8 %collective-permute-start.1 = (bf16[128,512]{1,0:T(8,128)(2,1)S(1)}, bf16[128,512]{1,0:T(8,128)(2,1)S(1)}, u32[]{:S(2)}, u32[]{:S(2)}) collective-permute-start(bf16[128,512]{1,0:T(8,128)(2,1)S(1)} %collective-permute-done), channel_id=1, source_target_pairs={{0,4},{4,8},{8,12},{12,0},{1,5},{5,9},{9,13},{13,1},{2,6},{6,10},{... | collective-permute-start | bytes 393224 | tf_op jit(solution)/shard_map/ppermute | solution.py:37
  9.7 9.4 %collective-permute-start.4 = (bf16[128,512]{1,0:T(8,128)(2,1)S(1)}, bf16[128,512]{1,0:T(8,128)(2,1)S(1)}, u32[]{:S(2)}, u32[]{:S(2)}) collective-permute-start(bf16[128,512]{1,0:T(8,128)(2,1)S(1)} %collective-permute-done), channel_id=1, source_target_pairs={{0,2},{2,0},{1,3},{3,1},{4,6},{6,4},{5,7},{7,5},{8,10},{10,8},{9,1... | collective-permute-start | bytes 393224 | tf_op jit(solution)/shard_map/ppermute | solution.py:37
  12.4 6.7 %collective-permute-start.6 = (bf16[128,512]{1,0:T(8,128)(2,1)S(1)}, bf16[128,512]{1,0:T(8,128)(2,1)S(1)}, u32[]{:S(2)}, u32[]{:S(2)}) collective-permute-start(bf16[128,512]{1,0:T(8,128)(2,1)S(1)} %collective-permute-done.3), channel_id=1, source_target_pairs={{0,2},{2,0},{1,3},{3,1},{4,6},{6,4},{5,7},{7,5},{8,10},{10,8},{9,1... | collective-permute-start | bytes 393224 | tf_op jit(solution)/shard_map/ppermute | solution.py:37
  16.5 5.4 %collective-permute-start.5 = (bf16[128,512]{1,0:T(8,128)(2,1)S(1)}, bf16[128,512]{1,0:T(8,128)(2,1)S(1)}, u32[]{:S(2)}, u32[]{:S(2)}) collective-permute-start(bf16[128,512]{1,0:T(8,128)(2,1)S(1)} %collective-permute-done.1), channel_id=1, source_target_pairs={{0,2},{2,0},{1,3},{3,1},{4,6},{6,4},{5,7},{7,5},{8,10},{10,8},{9,1... | collective-permute-start | bytes 393224 | tf_op jit(solution)/shard_map/ppermute | solution.py:37
  19.0 3.0 %collective-permute-start.7 = (bf16[4,128,512]{2,1,0:T(8,128)(2,1)S(1)}, bf16[4,128,512]{2,1,0:T(8,128)(2,1)S(1)}, u32[]{:S(2)}, u32[]{:S(2)}) collective-permute-start(bf16[4,128,512]{2,1,0:T(8,128)(2,1)S(1)} %pad_maximum_fusion.refs_4_), channel_id=1, source_target_pairs={{0,1},{1,0},{2,3},{3,2},{4,5},{5,4},{6,7},{7,6},{8,9},{9,8},{10,11... | collective-permute-start | bytes 1572872 | tf_op jit(solution)/shard_map/ppermute | solution.py:37
  21.9 2.0 %collective-permute-start.8 = (bf16[4,128,512]{2,1,0:T(8,128)(2,1)S(1)}, bf16[4,128,512]{2,1,0:T(8,128)(2,1)S(1)}, u32[]{:S(2)}, u32[]{:S(2)}) collective-permute-start(bf16[4,128,512]{2,1,0:T(8,128)(2,1)S(1)} %pad_maximum_fusion.1.refs_5_), channel_id=1, source_target_pairs={{0,1},{1,0},{2,3},{3,2},{4,5},{5,4},{6,7},{7,6},{8,9},{9,8},{10,11... | collective-permute-start | bytes 1572872 | tf_op jit(solution)/shard_map/ppermute | solution.py:37

commit v5 on v4

--- a/solution.py
+++ b/solution.py
@@ -12,7 +12,8 @@
 HALO = 16
 TILE = 256
 LANES = 128
-GROUP = 16
+GROUP = 32
+CHUNK = 4
 NEAR_CELLS = 2 << 20
 
 
@@ -92,7 +93,7 @@
 def correlate_body(*refs, near, cable_count, lag_devices, time_devices):
     dest_ref, space_ref, time_ref, code_ref = refs[:4]
     cable_refs = refs[4 : 4 + cable_count]
-    out_ref, raw_ref, smooth_ref, bank_ref, flip_ref, scale_ref, picked_ref, sems = refs[
+    out_ref, raw_ref, smooth_ref, bank_ref, flip_ref, scale_ref, partner_ref, picked_ref, sems = refs[
         4 + cable_count :
     ]
     tap_devices, block_taps, time_step = cable_refs[0].shape
@@ -179,10 +180,8 @@
             power = power + jnp.sum(white * white, axis=1, keepdims=True)
         energy = power / time_total + EPSILON
         inverse = jnp.broadcast_to(1.0 / jnp.sqrt(energy), (rows_all, LANES))
-        inverse_high, inverse_low = split_parts(inverse)
-        bank_ref[:, pl.ds(time_total, LANES)] = inverse_high
-        bank_ref[:, pl.ds(time_total + LANES, LANES)] = inverse_low
         scale_ref[...] = inverse[dest_rows:]
+        partner_ref[...] = inverse[:dest_rows].T[:8]
         at_row = lax.broadcasted_iota(jnp.int32, (2 * TILE, TILE), 0)
         at_col = lax.broadcasted_iota(jnp.int32, (2 * TILE, TILE), 1)
         mirror = (at_row + at_col == TILE).astype(jnp.bfloat16)
@@ -199,22 +198,30 @@
 
     columns = pltpu.roll(code_ref[...], lax.rem(LANES - step_id * GROUP, LANES), 1)
     at_lane = lax.broadcasted_iota(jnp.int32, (partner_count, dest_rows), 1).astype(jnp.float32)
-    chosen = jnp.concatenate(
-        [
-            (at_lane == columns[:, member : member + 1]).astype(jnp.bfloat16)
-            for member in range(GROUP)
-        ],
-        axis=0,
-    )
-    picked = jnp.dot(chosen, bank_ref[:dest_rows, :], preferred_element_type=jnp.float32)
-    picked_ref[...] = picked[:, :time_total].astype(jnp.bfloat16)
-    partner_scale = picked[:, time_total : time_total + LANES] + picked[:, time_total + LANES :]
+    hits = [at_lane == columns[:, member : member + 1] for member in range(GROUP)]
+
+    def pick(first):
+        members = slice(first, first + CHUNK)
+        chosen = jnp.concatenate([hit.astype(jnp.bfloat16) for hit in hits[members]], axis=0)
+        picked = jnp.dot(chosen, bank_ref[:dest_rows, :], preferred_element_type=jnp.float32)
+        rows = slice(first * partner_count, (first + CHUNK) * partner_count)
+        picked_ref[rows, :] = picked.astype(jnp.bfloat16)
+
+    pick(0)
     blank = jnp.zeros((LANES, LANES), jnp.bfloat16)
     window_scale = 1.0 / (float(time_total) ** 0.5)
     first_row = step_id * GROUP
+    def turned(member):
+        row = flip_ref[pl.ds(first_row + member, 1), :]
+        return shifted_rows(row.astype(jnp.bfloat16), LANES)
+
+    wides = [turned(0)]
     for member in range(GROUP):
-        row = flip_ref[pl.ds(first_row + member, 1), :]
-        wide = shifted_rows(row.astype(jnp.bfloat16), LANES)
+        if member % CHUNK == 0 and member + CHUNK < GROUP:
+            pick(member + CHUNK)
+        wide = wides[member]
+        if member + 1 < GROUP:
+            wides.append(turned(member + 1))
 
         def diagonal(k):
             if k < 0 or k > time_total // LANES:
@@ -243,8 +250,11 @@
             preferred_element_type=jnp.float32,
         )
         before, after = both[:partner_count], both[partner_count:]
-        scale = partner_scale[part] * scale_ref[pl.ds(first_row + member, 1), :] * window_scale
-        scale = jnp.concatenate([scale, scale], axis=1)
+        scale = jnp.sum(
+            jnp.where(hits[member], partner_ref[:1, :], 0.0), axis=1, keepdims=True
+        )
+        own_scale = scale_ref[pl.ds(first_row + member, 1), :] * window_scale
+        scale = scale * jnp.concatenate([own_scale, own_scale], axis=1)
         out_ref[0, member, :, :TILE] = (before * scale).astype(jnp.bfloat16)
         out_ref[0, member, :, TILE:] = (after * scale).astype(jnp.bfloat16)
 
@@ -296,9 +306,10 @@
             scratch_shapes=[
                 pltpu.VMEM((dest_count + 1, block_taps + 2 * HALO, time_total), jnp.bfloat16),
                 pltpu.VMEM((rows_all, wide), jnp.bfloat16),
-                pltpu.VMEM((rows_all, wide), jnp.bfloat16),
+                pltpu.VMEM((rows_all, time_total), jnp.bfloat16),
                 pltpu.VMEM((source_count, wide), jnp.float32),
                 pltpu.VMEM((source_count, LANES), jnp.float32),
+                pltpu.VMEM((8, dest_count * block_taps), jnp.float32),
                 pltpu.VMEM((GROUP * partner_count, time_total), jnp.bfloat16),
                 pltpu.SemaphoreType.DMA((dest_count + 1, 3 * time_devices)),
             ],

time: 37.6 us -> 36.8 us (0.979)
  Pallas kernels: 15.2 us -> 14.5 us
    pallas_call x1, Pallas kernels: 13.5 us -> 12.7 us  [per_device(): pl.pallas_call(body, grid_spec=pltpu.PrefetchScalarGridSpec(num_scalar_pr...]
where the time goes in v5:
time: 36.8 us; the launch traced here: 36.6 us
  Pallas kernels  14.5 us (39%)
  starting transfers between devices  13 us (35%)
  waiting for transfers between devices  7.97 us (22%)
  local copies, waits for them, and re-layouts  0.97 us (3%)
    ppermute x9, starting transfers between devices, shifted(): lax.ppermute(cells, axis, [(i, (i + step) % count) for i in range(count)])  13 us
    pallas_call x1, Pallas kernels, per_device(): pl.pallas_call(body, grid_spec=pltpu.PrefetchScalarGridSpec(num_scalar_pr...  12.7 us
    ppermute x9, waiting for transfers between devices, shifted(): lax.ppermute(cells, axis, [(i, (i + step) % count) for i in range(count)])  7.97 us
    pallas_call x1, Pallas kernels, per_device(): pl.pallas_call(functools.partial(bands_body, block_total=dest_blocks.shap...  1.79 us
    unnamed x2, local copies, waits for them, and re-layouts  0.95 us
  transfers between devices with their start and end apart: 9, of which 5 were waited for; matrix products, arithmetic and copies ran while one was open for 0% of the time, Pallas kernels for 5%

profile of v5, /device:TPU:0, one launch (start us, length us, event | category | flops | bytes accessed | tf_op | source)
XLA Modules:
  0.0 36.6 jit_solution(4425312242989575106)
XLA Ops:
  0.0 0.0 copy-start
  0.0 0.9 %copy-done = bf16[256,512]{1,0:T(8,128)(2,1)S(1)} copy-done((bf16[256,512]{1,0:T(8,128)(2,1)S(1)}, bf16[256,512]{1,0:T(8,128)(2,1)}, u32[]{:S(2)}) %copy-start) | copy-done | bytes 262168
  1.0 3.1 %collective-permute-start = (bf16[128,512]{1,0:T(8,128)(2,1)S(1)}, bf16[128,512]{1,0:T(8,128)(2,1)S(1)}, u32[]{:S(2)}, u32[]{:S(2)}) collective-permute-start(bf16[128,512]{1,0:T(8,128)(2,1)S(1)} %constant_dynamic-slice_fusion), channel_id=1, source_target_pairs={{0,4},{4,8},{8,12},{12,0},{1,5},{5,9},{9,13},{13,1},{2,6},{6,10},{... | collective-permute-start | bytes 393224 | tf_op jit(solution)/shard_map/ppermute | solution.py:38
  4.0 1.5 %collective-permute-start.2 = (bf16[128,512]{1,0:T(8,128)(2,1)S(1)}, bf16[128,512]{1,0:T(8,128)(2,1)S(1)}, u32[]{:S(2)}, u32[]{:S(2)}) collective-permute-start(bf16[128,512]{1,0:T(8,128)(2,1)S(1)} %constant_dynamic-slice_fusion), channel_id=1, source_target_pairs={{0,2},{2,0},{1,3},{3,1},{4,6},{6,4},{5,7},{7,5},{8,10},{10,8},{9,1... | collective-permute-start | bytes 393224 | tf_op jit(solution)/shard_map/ppermute | solution.py:38
  5.5 2.2 %collective-permute-start.3 = (bf16[128,512]{1,0:T(8,128)(2,1)S(1)}, bf16[128,512]{1,0:T(8,128)(2,1)S(1)}, u32[]{:S(2)}, u32[]{:S(2)}) collective-permute-start(bf16[128,512]{1,0:T(8,128)(2,1)S(1)} %constant_dynamic-slice_fusion), channel_id=1, source_target_pairs={{0,12},{4,0},{8,4},{12,8},{1,13},{5,1},{9,5},{13,9},{2,14},{6,2},{... | collective-permute-start | bytes 393224 | tf_op jit(solution)/shard_map/ppermute | solution.py:38
  7.8 1.8 %shard_map.55 = (bf16[2,320,160]{2,1,0:T(8,128)(2,1)S(1)}, bf16[2,512,256]{2,1,0:T(8,128)(2,1)S(1)}, f32[64,128]{1,0:T(8,128)S(1)}) custom-call(s32[2,8]{1,0:T(2,128)} %bitcast.17, s32[1,64,64]{2,1,0:T(8,128)} %codes_ref.1, f32[33]{0:T(128)} %space_ref.1, f32[255]{0:T(256)} %time_ref.1), custom_call_target="tpu_custom_call" | custom-call | tf_op jit(solution)/shard_map/pallas_call | solution.py:272
  9.6 0.1 collective-permute-done
  9.7 0.0 collective-permute-start.1
  9.7 2.4 %collective-permute-start.4 = (bf16[128,512]{1,0:T(8,128)(2,1)S(1)}, bf16[128,512]{1,0:T(8,128)(2,1)S(1)}, u32[]{:S(2)}, u32[]{:S(2)}) collective-permute-start(bf16[128,512]{1,0:T(8,128)(2,1)S(1)} %collective-permute-done), channel_id=1, source_target_pairs={{0,2},{2,0},{1,3},{3,1},{4,6},{6,4},{5,7},{7,5},{8,10},{10,8},{9,1... | collective-permute-start | bytes 393224 | tf_op jit(solution)/shard_map/ppermute | solution.py:38
  12.1 0.2 collective-permute-done.3
  12.4 1.2 %collective-permute-start.6 = (bf16[128,512]{1,0:T(8,128)(2,1)S(1)}, bf16[128,512]{1,0:T(8,128)(2,1)S(1)}, u32[]{:S(2)}, u32[]{:S(2)}) collective-permute-start(bf16[128,512]{1,0:T(8,128)(2,1)S(1)} %collective-permute-done.3), channel_id=1, source_target_pairs={{0,2},{2,0},{1,3},{3,1},{4,6},{6,4},{5,7},{7,5},{8,10},{10,8},{9,1... | collective-permute-start | bytes 393224 | tf_op jit(solution)/shard_map/ppermute | solution.py:38
  13.6 0.0 collective-permute-done.2
  13.6 2.9 %collective-permute-done.1 = bf16[128,512]{1,0:T(8,128)(2,1)S(1)} collective-permute-done((bf16[128,512]{1,0:T(8,128)(2,1)S(1)}, bf16[128,512]{1,0:T(8,128)(2,1)S(1)}, u32[]{:S(2)}, u32[]{:S(2)}) %collective-permute-start.1) | collective-permute-done | bytes 131104 | tf_op jit(solution)/shard_map/ppermute | solution.py:38
  16.5 2.4 %collective-permute-start.5 = (bf16[128,512]{1,0:T(8,128)(2,1)S(1)}, bf16[128,512]{1,0:T(8,128)(2,1)S(1)}, u32[]{:S(2)}, u32[]{:S(2)}) collective-permute-start(bf16[128,512]{1,0:T(8,128)(2,1)S(1)} %collective-permute-done.1), channel_id=1, source_target_pairs={{0,2},{2,0},{1,3},{3,1},{4,6},{6,4},{5,7},{7,5},{8,10},{10,8},{9,1... | collective-permute-start | bytes 393224 | tf_op jit(solution)/shard_map/ppermute | solution.py:38
  18.9 0.1 pad_maximum_fusion.refs_4_
  19.0 0.1 collective-permute-start.7
  19.1 0.0 collective-permute-done.6
  19.1 0.0 collective-permute-done.4
  19.1 2.8 %collective-permute-done.5 = bf16[128,512]{1,0:T(8,128)(2,1)S(1)} collective-permute-done((bf16[128,512]{1,0:T(8,128)(2,1)S(1)}, bf16[128,512]{1,0:T(8,128)(2,1)S(1)}, u32[]{:S(2)}, u32[]{:S(2)}) %collective-permute-start.5) | collective-permute-done | bytes 131104 | tf_op jit(solution)/shard_map/ppermute | solution.py:38
  21.8 0.1 pad_maximum_fusion.1.refs_5_
  21.9 0.1 collective-permute-start.8
  22.0 0.0 collective-permute-done.7.refs_6_
  22.0 1.9 %collective-permute-done.8.refs_7_ = bf16[4,128,512]{2,1,0:T(8,128)(2,1)S(1)} collective-permute-done((bf16[4,128,512]{2,1,0:T(8,128)(2,1)S(1)}, bf16[4,128,512]{2,1,0:T(8,128)(2,1)S(1)}, u32[]{:S(2)}, u32[]{:S(2)}) %collective-permute-start.8) | collective-permute-done | bytes 524320 | tf_op jit(solution)/shard_map/ppermute | solution.py:38
  23.9 12.7 %shard_map.56 = bf16[1,64,64,512]{3,2,1,0:T(8,128)(2,1)} custom-call(s32[2,8]{1,0:T(2,128)} %bitcast.18, bf16[2,320,160]{2,1,0:T(8,128)(2,1)S(1)} %get-tuple-element.17.refs_1_, bf16[2,512,256]{2,1,0:T(8,128)(2,1)S(1)} %get-tuple-element.18.refs_2_, f32[64,128]{1,0:T(8,128)S(1)} %get-tuple-element.19.refs_3_, ...), custom_call_target="tpu_custom_call" | custom-call | tf_op jit(solution)/shard_map/pallas_call | solution.py:299
  (2 shorter events, 0.0 us)
Async XLA Ops:
  0.0 1.0 %copy-start = (bf16[256,512]{1,0:T(8,128)(2,1)S(1)}, bf16[256,512]{1,0:T(8,128)(2,1)}, u32[]{:S(2)}) copy-start(bf16[256,512]{1,0:T(8,128)(2,1)} %param.5) | copy-start | bytes 786436
  1.0 8.8 %collective-permute-start = (bf16[128,512]{1,0:T(8,128)(2,1)S(1)}, bf16[128,512]{1,0:T(8,128)(2,1)S(1)}, u32[]{:S(2)}, u32[]{:S(2)}) collective-permute-start(bf16[128,512]{1,0:T(8,128)(2,1)S(1)} %constant_dynamic-slice_fusion), channel_id=1, source_target_pairs={{0,4},{4,8},{8,12},{12,0},{1,5},{5,9},{9,13},{13,1},{2,6},{6,10},{... | collective-permute-start | bytes 393224 | tf_op jit(solution)/shard_map/ppermute | solution.py:38
  4.0 9.5 %collective-permute-start.2 = (bf16[128,512]{1,0:T(8,128)(2,1)S(1)}, bf16[128,512]{1,0:T(8,128)(2,1)S(1)}, u32[]{:S(2)}, u32[]{:S(2)}) collective-permute-start(bf16[128,512]{1,0:T(8,128)(2,1)S(1)} %constant_dynamic-slice_fusion), channel_id=1, source_target_pairs={{0,2},{2,0},{1,3},{3,1},{4,6},{6,4},{5,7},{7,5},{8,10},{10,8},{9,1... | collective-permute-start | bytes 393224 | tf_op jit(solution)/shard_map/ppermute | solution.py:38
  5.5 6.8 %collective-permute-start.3 = (bf16[128,512]{1,0:T(8,128)(2,1)S(1)}, bf16[128,512]{1,0:T(8,128)(2,1)S(1)}, u32[]{:S(2)}, u32[]{:S(2)}) collective-permute-start(bf16[128,512]{1,0:T(8,128)(2,1)S(1)} %constant_dynamic-slice_fusion), channel_id=1, source_target_pairs={{0,12},{4,0},{8,4},{12,8},{1,13},{5,1},{9,5},{13,9},{2,14},{6,2},{... | collective-permute-start | bytes 393224 | tf_op jit(solution)/shard_map/ppermute | solution.py:38
  9.7 6.8 %collective-permute-start.1 = (bf16[128,512]{1,0:T(8,128)(2,1)S(1)}, bf16[128,512]{1,0:T(8,128)(2,1)S(1)}, u32[]{:S(2)}, u32[]{:S(2)}) collective-permute-start(bf16[128,512]{1,0:T(8,128)(2,1)S(1)} %collective-permute-done), channel_id=1, source_target_pairs={{0,4},{4,8},{8,12},{12,0},{1,5},{5,9},{9,13},{13,1},{2,6},{6,10},{... | collective-permute-start | bytes 393224 | tf_op jit(solution)/shard_map/ppermute | solution.py:38
  9.7 9.4 %collective-permute-start.4 = (bf16[128,512]{1,0:T(8,128)(2,1)S(1)}, bf16[128,512]{1,0:T(8,128)(2,1)S(1)}, u32[]{:S(2)}, u32[]{:S(2)}) collective-permute-start(bf16[128,512]{1,0:T(8,128)(2,1)S(1)} %collective-permute-done), channel_id=1, source_target_pairs={{0,2},{2,0},{1,3},{3,1},{4,6},{6,4},{5,7},{7,5},{8,10},{10,8},{9,1... | collective-permute-start | bytes 393224 | tf_op jit(solution)/shard_map/ppermute | solution.py:38
  12.4 6.7 %collective-permute-start.6 = (bf16[128,512]{1,0:T(8,128)(2,1)S(1)}, bf16[128,512]{1,0:T(8,128)(2,1)S(1)}, u32[]{:S(2)}, u32[]{:S(2)}) collective-permute-start(bf16[128,512]{1,0:T(8,128)(2,1)S(1)} %collective-permute-done.3), channel_id=1, source_target_pairs={{0,2},{2,0},{1,3},{3,1},{4,6},{6,4},{5,7},{7,5},{8,10},{10,8},{9,1... | collective-permute-start | bytes 393224 | tf_op jit(solution)/shard_map/ppermute | solution.py:38
  16.5 5.4 %collective-permute-start.5 = (bf16[128,512]{1,0:T(8,128)(2,1)S(1)}, bf16[128,512]{1,0:T(8,128)(2,1)S(1)}, u32[]{:S(2)}, u32[]{:S(2)}) collective-permute-start(bf16[128,512]{1,0:T(8,128)(2,1)S(1)} %collective-permute-done.1), channel_id=1, source_target_pairs={{0,2},{2,0},{1,3},{3,1},{4,6},{6,4},{5,7},{7,5},{8,10},{10,8},{9,1... | collective-permute-start | bytes 393224 | tf_op jit(solution)/shard_map/ppermute | solution.py:38
  19.0 3.0 %collective-permute-start.7 = (bf16[4,128,512]{2,1,0:T(8,128)(2,1)S(1)}, bf16[4,128,512]{2,1,0:T(8,128)(2,1)S(1)}, u32[]{:S(2)}, u32[]{:S(2)}) collective-permute-start(bf16[4,128,512]{2,1,0:T(8,128)(2,1)S(1)} %pad_maximum_fusion.refs_4_), channel_id=1, source_target_pairs={{0,1},{1,0},{2,3},{3,2},{4,5},{5,4},{6,7},{7,6},{8,9},{9,8},{10,11... | collective-permute-start | bytes 1572872 | tf_op jit(solution)/shard_map/ppermute | solution.py:38
  21.9 2.0 %collective-permute-start.8 = (bf16[4,128,512]{2,1,0:T(8,128)(2,1)S(1)}, bf16[4,128,512]{2,1,0:T(8,128)(2,1)S(1)}, u32[]{:S(2)}, u32[]{:S(2)}) collective-permute-start(bf16[4,128,512]{2,1,0:T(8,128)(2,1)S(1)} %pad_maximum_fusion.1.refs_5_), channel_id=1, source_target_pairs={{0,1},{1,0},{2,3},{3,2},{4,5},{5,4},{6,7},{7,6},{8,9},{9,8},{10,11... | collective-permute-start | bytes 1572872 | tf_op jit(solution)/shard_map/ppermute | solution.py:38

commit v6 on v5

--- a/solution.py
+++ b/solution.py
@@ -13,7 +13,7 @@
 TILE = 256
 LANES = 128
 GROUP = 32
-CHUNK = 4
+CHUNK = 16
 NEAR_CELLS = 2 << 20
 
 
@@ -172,8 +172,11 @@
         power = jnp.zeros((rows_all, 1), jnp.float32)
         for tile in range(tiles):
             window = smooth_ref[:, tile * TILE : tile * TILE + 2 * TILE]
-            white = jnp.dot(window, time_ref[0], preferred_element_type=jnp.float32)
-            white = white + jnp.dot(window, time_ref[1], preferred_element_type=jnp.float32)
+            white = jnp.dot(
+                jnp.concatenate([window, window], axis=1),
+                time_ref[...].reshape(4 * TILE, TILE),
+                preferred_element_type=jnp.float32,
+            )
             white = white.astype(jnp.bfloat16)
             bank_ref[:, tile * TILE : (tile + 1) * TILE] = white
             white = white.astype(jnp.float32)

time: 36.8 us -> 36.8 us (level)
  no operation moved by 1% of the time
where the time goes in v6:
time: 36.8 us; the launch traced here: 36.6 us
  Pallas kernels  14.5 us (39%)
  starting transfers between devices  13 us (35%)
  waiting for transfers between devices  7.97 us (22%)
  local copies, waits for them, and re-layouts  0.97 us (3%)
    ppermute x9, starting transfers between devices, shifted(): lax.ppermute(cells, axis, [(i, (i + step) % count) for i in range(count)])  13 us
    pallas_call x1, Pallas kernels, per_device(): pl.pallas_call(body, grid_spec=pltpu.PrefetchScalarGridSpec(num_scalar_pr...  12.7 us
    ppermute x9, waiting for transfers between devices, shifted(): lax.ppermute(cells, axis, [(i, (i + step) % count) for i in range(count)])  7.97 us
    pallas_call x1, Pallas kernels, per_device(): pl.pallas_call(functools.partial(bands_body, block_total=dest_blocks.shap...  1.79 us
    unnamed x2, local copies, waits for them, and re-layouts  0.95 us
  transfers between devices with their start and end apart: 9, of which 5 were waited for; matrix products, arithmetic and copies ran while one was open for 0% of the time, Pallas kernels for 5%

profile of v6, /device:TPU:0, one launch (start us, length us, event | category | flops | bytes accessed | tf_op | source)
XLA Modules:
  0.0 36.6 jit_solution(7634691353997444125)
XLA Ops:
  0.0 0.0 copy-start
  0.0 0.9 %copy-done = bf16[256,512]{1,0:T(8,128)(2,1)S(1)} copy-done((bf16[256,512]{1,0:T(8,128)(2,1)S(1)}, bf16[256,512]{1,0:T(8,128)(2,1)}, u32[]{:S(2)}) %copy-start) | copy-done | bytes 262168
  1.0 3.1 %collective-permute-start = (bf16[128,512]{1,0:T(8,128)(2,1)S(1)}, bf16[128,512]{1,0:T(8,128)(2,1)S(1)}, u32[]{:S(2)}, u32[]{:S(2)}) collective-permute-start(bf16[128,512]{1,0:T(8,128)(2,1)S(1)} %constant_dynamic-slice_fusion), channel_id=1, source_target_pairs={{0,4},{4,8},{8,12},{12,0},{1,5},{5,9},{9,13},{13,1},{2,6},{6,10},{... | collective-permute-start | bytes 393224 | tf_op jit(solution)/shard_map/ppermute | solution.py:38
  4.0 1.5 %collective-permute-start.2 = (bf16[128,512]{1,0:T(8,128)(2,1)S(1)}, bf16[128,512]{1,0:T(8,128)(2,1)S(1)}, u32[]{:S(2)}, u32[]{:S(2)}) collective-permute-start(bf16[128,512]{1,0:T(8,128)(2,1)S(1)} %constant_dynamic-slice_fusion), channel_id=1, source_target_pairs={{0,2},{2,0},{1,3},{3,1},{4,6},{6,4},{5,7},{7,5},{8,10},{10,8},{9,1... | collective-permute-start | bytes 393224 | tf_op jit(solution)/shard_map/ppermute | solution.py:38
  5.5 2.2 %collective-permute-start.3 = (bf16[128,512]{1,0:T(8,128)(2,1)S(1)}, bf16[128,512]{1,0:T(8,128)(2,1)S(1)}, u32[]{:S(2)}, u32[]{:S(2)}) collective-permute-start(bf16[128,512]{1,0:T(8,128)(2,1)S(1)} %constant_dynamic-slice_fusion), channel_id=1, source_target_pairs={{0,12},{4,0},{8,4},{12,8},{1,13},{5,1},{9,5},{13,9},{2,14},{6,2},{... | collective-permute-start | bytes 393224 | tf_op jit(solution)/shard_map/ppermute | solution.py:38
  7.8 1.8 %shard_map.55 = (bf16[2,320,160]{2,1,0:T(8,128)(2,1)S(1)}, bf16[2,512,256]{2,1,0:T(8,128)(2,1)S(1)}, f32[64,128]{1,0:T(8,128)S(1)}) custom-call(s32[2,8]{1,0:T(2,128)} %bitcast.17, s32[1,64,64]{2,1,0:T(8,128)} %codes_ref.1, f32[33]{0:T(128)} %space_ref.1, f32[255]{0:T(256)} %time_ref.1), custom_call_target="tpu_custom_call" | custom-call | tf_op jit(solution)/shard_map/pallas_call | solution.py:275
  9.6 0.1 collective-permute-done
  9.7 0.0 collective-permute-start.1
  9.7 2.4 %collective-permute-start.4 = (bf16[128,512]{1,0:T(8,128)(2,1)S(1)}, bf16[128,512]{1,0:T(8,128)(2,1)S(1)}, u32[]{:S(2)}, u32[]{:S(2)}) collective-permute-start(bf16[128,512]{1,0:T(8,128)(2,1)S(1)} %collective-permute-done), channel_id=1, source_target_pairs={{0,2},{2,0},{1,3},{3,1},{4,6},{6,4},{5,7},{7,5},{8,10},{10,8},{9,1... | collective-permute-start | bytes 393224 | tf_op jit(solution)/shard_map/ppermute | solution.py:38
  12.1 0.2 collective-permute-done.3
  12.4 1.2 %collective-permute-start.6 = (bf16[128,512]{1,0:T(8,128)(2,1)S(1)}, bf16[128,512]{1,0:T(8,128)(2,1)S(1)}, u32[]{:S(2)}, u32[]{:S(2)}) collective-permute-start(bf16[128,512]{1,0:T(8,128)(2,1)S(1)} %collective-permute-done.3), channel_id=1, source_target_pairs={{0,2},{2,0},{1,3},{3,1},{4,6},{6,4},{5,7},{7,5},{8,10},{10,8},{9,1... | collective-permute-start | bytes 393224 | tf_op jit(solution)/shard_map/ppermute | solution.py:38
  13.6 0.0 collective-permute-done.2
  13.6 2.9 %collective-permute-done.1 = bf16[128,512]{1,0:T(8,128)(2,1)S(1)} collective-permute-done((bf16[128,512]{1,0:T(8,128)(2,1)S(1)}, bf16[128,512]{1,0:T(8,128)(2,1)S(1)}, u32[]{:S(2)}, u32[]{:S(2)}) %collective-permute-start.1) | collective-permute-done | bytes 131104 | tf_op jit(solution)/shard_map/ppermute | solution.py:38
  16.5 2.4 %collective-permute-start.5 = (bf16[128,512]{1,0:T(8,128)(2,1)S(1)}, bf16[128,512]{1,0:T(8,128)(2,1)S(1)}, u32[]{:S(2)}, u32[]{:S(2)}) collective-permute-start(bf16[128,512]{1,0:T(8,128)(2,1)S(1)} %collective-permute-done.1), channel_id=1, source_target_pairs={{0,2},{2,0},{1,3},{3,1},{4,6},{6,4},{5,7},{7,5},{8,10},{10,8},{9,1... | collective-permute-start | bytes 393224 | tf_op jit(solution)/shard_map/ppermute | solution.py:38
  18.9 0.1 pad_maximum_fusion.refs_4_
  19.0 0.1 collective-permute-start.7
  19.1 0.0 collective-permute-done.6
  19.1 0.0 collective-permute-done.4
  19.1 2.8 %collective-permute-done.5 = bf16[128,512]{1,0:T(8,128)(2,1)S(1)} collective-permute-done((bf16[128,512]{1,0:T(8,128)(2,1)S(1)}, bf16[128,512]{1,0:T(8,128)(2,1)S(1)}, u32[]{:S(2)}, u32[]{:S(2)}) %collective-permute-start.5) | collective-permute-done | bytes 131104 | tf_op jit(solution)/shard_map/ppermute | solution.py:38
  21.8 0.1 pad_maximum_fusion.1.refs_5_
  21.9 0.1 collective-permute-start.8
  22.0 0.0 collective-permute-done.7.refs_6_
  22.0 1.9 %collective-permute-done.8.refs_7_ = bf16[4,128,512]{2,1,0:T(8,128)(2,1)S(1)} collective-permute-done((bf16[4,128,512]{2,1,0:T(8,128)(2,1)S(1)}, bf16[4,128,512]{2,1,0:T(8,128)(2,1)S(1)}, u32[]{:S(2)}, u32[]{:S(2)}) %collective-permute-start.8) | collective-permute-done | bytes 524320 | tf_op jit(solution)/shard_map/ppermute | solution.py:38
  23.9 12.7 %shard_map.56 = bf16[1,64,64,512]{3,2,1,0:T(8,128)(2,1)} custom-call(s32[2,8]{1,0:T(2,128)} %bitcast.18, bf16[2,320,160]{2,1,0:T(8,128)(2,1)S(1)} %get-tuple-element.17.refs_1_, bf16[2,512,256]{2,1,0:T(8,128)(2,1)S(1)} %get-tuple-element.18.refs_2_, f32[64,128]{1,0:T(8,128)S(1)} %get-tuple-element.19.refs_3_, ...), custom_call_target="tpu_custom_call" | custom-call | tf_op jit(solution)/shard_map/pallas_call | solution.py:302
  (2 shorter events, 0.0 us)
Async XLA Ops:
  0.0 1.0 %copy-start = (bf16[256,512]{1,0:T(8,128)(2,1)S(1)}, bf16[256,512]{1,0:T(8,128)(2,1)}, u32[]{:S(2)}) copy-start(bf16[256,512]{1,0:T(8,128)(2,1)} %param.5) | copy-start | bytes 786436
  1.0 8.8 %collective-permute-start = (bf16[128,512]{1,0:T(8,128)(2,1)S(1)}, bf16[128,512]{1,0:T(8,128)(2,1)S(1)}, u32[]{:S(2)}, u32[]{:S(2)}) collective-permute-start(bf16[128,512]{1,0:T(8,128)(2,1)S(1)} %constant_dynamic-slice_fusion), channel_id=1, source_target_pairs={{0,4},{4,8},{8,12},{12,0},{1,5},{5,9},{9,13},{13,1},{2,6},{6,10},{... | collective-permute-start | bytes 393224 | tf_op jit(solution)/shard_map/ppermute | solution.py:38
  4.0 9.5 %collective-permute-start.2 = (bf16[128,512]{1,0:T(8,128)(2,1)S(1)}, bf16[128,512]{1,0:T(8,128)(2,1)S(1)}, u32[]{:S(2)}, u32[]{:S(2)}) collective-permute-start(bf16[128,512]{1,0:T(8,128)(2,1)S(1)} %constant_dynamic-slice_fusion), channel_id=1, source_target_pairs={{0,2},{2,0},{1,3},{3,1},{4,6},{6,4},{5,7},{7,5},{8,10},{10,8},{9,1... | collective-permute-start | bytes 393224 | tf_op jit(solution)/shard_map/ppermute | solution.py:38
  5.5 6.8 %collective-permute-start.3 = (bf16[128,512]{1,0:T(8,128)(2,1)S(1)}, bf16[128,512]{1,0:T(8,128)(2,1)S(1)}, u32[]{:S(2)}, u32[]{:S(2)}) collective-permute-start(bf16[128,512]{1,0:T(8,128)(2,1)S(1)} %constant_dynamic-slice_fusion), channel_id=1, source_target_pairs={{0,12},{4,0},{8,4},{12,8},{1,13},{5,1},{9,5},{13,9},{2,14},{6,2},{... | collective-permute-start | bytes 393224 | tf_op jit(solution)/shard_map/ppermute | solution.py:38
  9.7 6.8 %collective-permute-start.1 = (bf16[128,512]{1,0:T(8,128)(2,1)S(1)}, bf16[128,512]{1,0:T(8,128)(2,1)S(1)}, u32[]{:S(2)}, u32[]{:S(2)}) collective-permute-start(bf16[128,512]{1,0:T(8,128)(2,1)S(1)} %collective-permute-done), channel_id=1, source_target_pairs={{0,4},{4,8},{8,12},{12,0},{1,5},{5,9},{9,13},{13,1},{2,6},{6,10},{... | collective-permute-start | bytes 393224 | tf_op jit(solution)/shard_map/ppermute | solution.py:38
  9.7 9.4 %collective-permute-start.4 = (bf16[128,512]{1,0:T(8,128)(2,1)S(1)}, bf16[128,512]{1,0:T(8,128)(2,1)S(1)}, u32[]{:S(2)}, u32[]{:S(2)}) collective-permute-start(bf16[128,512]{1,0:T(8,128)(2,1)S(1)} %collective-permute-done), channel_id=1, source_target_pairs={{0,2},{2,0},{1,3},{3,1},{4,6},{6,4},{5,7},{7,5},{8,10},{10,8},{9,1... | collective-permute-start | bytes 393224 | tf_op jit(solution)/shard_map/ppermute | solution.py:38
  12.4 6.7 %collective-permute-start.6 = (bf16[128,512]{1,0:T(8,128)(2,1)S(1)}, bf16[128,512]{1,0:T(8,128)(2,1)S(1)}, u32[]{:S(2)}, u32[]{:S(2)}) collective-permute-start(bf16[128,512]{1,0:T(8,128)(2,1)S(1)} %collective-permute-done.3), channel_id=1, source_target_pairs={{0,2},{2,0},{1,3},{3,1},{4,6},{6,4},{5,7},{7,5},{8,10},{10,8},{9,1... | collective-permute-start | bytes 393224 | tf_op jit(solution)/shard_map/ppermute | solution.py:38
  16.5 5.4 %collective-permute-start.5 = (bf16[128,512]{1,0:T(8,128)(2,1)S(1)}, bf16[128,512]{1,0:T(8,128)(2,1)S(1)}, u32[]{:S(2)}, u32[]{:S(2)}) collective-permute-start(bf16[128,512]{1,0:T(8,128)(2,1)S(1)} %collective-permute-done.1), channel_id=1, source_target_pairs={{0,2},{2,0},{1,3},{3,1},{4,6},{6,4},{5,7},{7,5},{8,10},{10,8},{9,1... | collective-permute-start | bytes 393224 | tf_op jit(solution)/shard_map/ppermute | solution.py:38
  19.0 3.0 %collective-permute-start.7 = (bf16[4,128,512]{2,1,0:T(8,128)(2,1)S(1)}, bf16[4,128,512]{2,1,0:T(8,128)(2,1)S(1)}, u32[]{:S(2)}, u32[]{:S(2)}) collective-permute-start(bf16[4,128,512]{2,1,0:T(8,128)(2,1)S(1)} %pad_maximum_fusion.refs_4_), channel_id=1, source_target_pairs={{0,1},{1,0},{2,3},{3,2},{4,5},{5,4},{6,7},{7,6},{8,9},{9,8},{10,11... | collective-permute-start | bytes 1572872 | tf_op jit(solution)/shard_map/ppermute | solution.py:38
  21.9 2.0 %collective-permute-start.8 = (bf16[4,128,512]{2,1,0:T(8,128)(2,1)S(1)}, bf16[4,128,512]{2,1,0:T(8,128)(2,1)S(1)}, u32[]{:S(2)}, u32[]{:S(2)}) collective-permute-start(bf16[4,128,512]{2,1,0:T(8,128)(2,1)S(1)} %pad_maximum_fusion.1.refs_5_), channel_id=1, source_target_pairs={{0,1},{1,0},{2,3},{3,2},{4,5},{5,4},{6,7},{7,6},{8,9},{9,8},{10,11... | collective-permute-start | bytes 1572872 | tf_op jit(solution)/shard_map/ppermute | solution.py:38

commit v7 on v5

--- a/solution.py
+++ b/solution.py
@@ -13,7 +13,7 @@
 TILE = 256
 LANES = 128
 GROUP = 32
-CHUNK = 4
+CHUNK = 8
 NEAR_CELLS = 2 << 20
 
 
@@ -211,17 +211,11 @@
     blank = jnp.zeros((LANES, LANES), jnp.bfloat16)
     window_scale = 1.0 / (float(time_total) ** 0.5)
     first_row = step_id * GROUP
-    def turned(member):
-        row = flip_ref[pl.ds(first_row + member, 1), :]
-        return shifted_rows(row.astype(jnp.bfloat16), LANES)
-
-    wides = [turned(0)]
     for member in range(GROUP):
         if member % CHUNK == 0 and member + CHUNK < GROUP:
             pick(member + CHUNK)
-        wide = wides[member]
-        if member + 1 < GROUP:
-            wides.append(turned(member + 1))
+        row = flip_ref[pl.ds(first_row + member, 1), :]
+        wide = shifted_rows(row.astype(jnp.bfloat16), LANES)
 
         def diagonal(k):
             if k < 0 or k > time_total // LANES:

time: 36.8 us -> 36.8 us (level)
  no operation moved by 1% of the time
where the time goes in v7:
time: 36.8 us; the launch traced here: 36.5 us
  Pallas kernels  14.4 us (39%)
  starting transfers between devices  13 us (35%)
  waiting for transfers between devices  7.97 us (22%)
  local copies, waits for them, and re-layouts  0.97 us (3%)
    ppermute x9, starting transfers between devices, shifted(): lax.ppermute(cells, axis, [(i, (i + step) % count) for i in range(count)])  13 us
    pallas_call x1, Pallas kernels, per_device(): pl.pallas_call(body, grid_spec=pltpu.PrefetchScalarGridSpec(num_scalar_pr...  12.6 us
    ppermute x9, waiting for transfers between devices, shifted(): lax.ppermute(cells, axis, [(i, (i + step) % count) for i in range(count)])  7.97 us
    pallas_call x1, Pallas kernels, per_device(): pl.pallas_call(functools.partial(bands_body, block_total=dest_blocks.shap...  1.79 us
    unnamed x2, local copies, waits for them, and re-layouts  0.95 us
  transfers between devices with their start and end apart: 9, of which 5 were waited for; matrix products, arithmetic and copies ran while one was open for 0% of the time, Pallas kernels for 5%

profile of v7, /device:TPU:0, one launch (start us, length us, event | category | flops | bytes accessed | tf_op | source)
XLA Modules:
  0.0 36.5 jit_solution(15297170938590677385)
XLA Ops:
  0.0 0.0 copy-start
  0.0 0.9 %copy-done = bf16[256,512]{1,0:T(8,128)(2,1)S(1)} copy-done((bf16[256,512]{1,0:T(8,128)(2,1)S(1)}, bf16[256,512]{1,0:T(8,128)(2,1)}, u32[]{:S(2)}) %copy-start) | copy-done | bytes 262168
  1.0 3.1 %collective-permute-start = (bf16[128,512]{1,0:T(8,128)(2,1)S(1)}, bf16[128,512]{1,0:T(8,128)(2,1)S(1)}, u32[]{:S(2)}, u32[]{:S(2)}) collective-permute-start(bf16[128,512]{1,0:T(8,128)(2,1)S(1)} %constant_dynamic-slice_fusion), channel_id=1, source_target_pairs={{0,4},{4,8},{8,12},{12,0},{1,5},{5,9},{9,13},{13,1},{2,6},{6,10},{... | collective-permute-start | bytes 393224 | tf_op jit(solution)/shard_map/ppermute | solution.py:38
  4.0 1.5 %collective-permute-start.2 = (bf16[128,512]{1,0:T(8,128)(2,1)S(1)}, bf16[128,512]{1,0:T(8,128)(2,1)S(1)}, u32[]{:S(2)}, u32[]{:S(2)}) collective-permute-start(bf16[128,512]{1,0:T(8,128)(2,1)S(1)} %constant_dynamic-slice_fusion), channel_id=1, source_target_pairs={{0,2},{2,0},{1,3},{3,1},{4,6},{6,4},{5,7},{7,5},{8,10},{10,8},{9,1... | collective-permute-start | bytes 393224 | tf_op jit(solution)/shard_map/ppermute | solution.py:38
  5.5 2.2 %collective-permute-start.3 = (bf16[128,512]{1,0:T(8,128)(2,1)S(1)}, bf16[128,512]{1,0:T(8,128)(2,1)S(1)}, u32[]{:S(2)}, u32[]{:S(2)}) collective-permute-start(bf16[128,512]{1,0:T(8,128)(2,1)S(1)} %constant_dynamic-slice_fusion), channel_id=1, source_target_pairs={{0,12},{4,0},{8,4},{12,8},{1,13},{5,1},{9,5},{13,9},{2,14},{6,2},{... | collective-permute-start | bytes 393224 | tf_op jit(solution)/shard_map/ppermute | solution.py:38
  7.8 1.8 %shard_map.55 = (bf16[2,320,160]{2,1,0:T(8,128)(2,1)S(1)}, bf16[2,512,256]{2,1,0:T(8,128)(2,1)S(1)}, f32[64,128]{1,0:T(8,128)S(1)}) custom-call(s32[2,8]{1,0:T(2,128)} %bitcast.17, s32[1,64,64]{2,1,0:T(8,128)} %codes_ref.1, f32[33]{0:T(128)} %space_ref.1, f32[255]{0:T(256)} %time_ref.1), custom_call_target="tpu_custom_call" | custom-call | tf_op jit(solution)/shard_map/pallas_call | solution.py:266
  9.6 0.1 collective-permute-done
  9.7 0.0 collective-permute-start.1
  9.7 2.4 %collective-permute-start.4 = (bf16[128,512]{1,0:T(8,128)(2,1)S(1)}, bf16[128,512]{1,0:T(8,128)(2,1)S(1)}, u32[]{:S(2)}, u32[]{:S(2)}) collective-permute-start(bf16[128,512]{1,0:T(8,128)(2,1)S(1)} %collective-permute-done), channel_id=1, source_target_pairs={{0,2},{2,0},{1,3},{3,1},{4,6},{6,4},{5,7},{7,5},{8,10},{10,8},{9,1... | collective-permute-start | bytes 393224 | tf_op jit(solution)/shard_map/ppermute | solution.py:38
  12.1 0.2 collective-permute-done.3
  12.4 1.2 %collective-permute-start.6 = (bf16[128,512]{1,0:T(8,128)(2,1)S(1)}, bf16[128,512]{1,0:T(8,128)(2,1)S(1)}, u32[]{:S(2)}, u32[]{:S(2)}) collective-permute-start(bf16[128,512]{1,0:T(8,128)(2,1)S(1)} %collective-permute-done.3), channel_id=1, source_target_pairs={{0,2},{2,0},{1,3},{3,1},{4,6},{6,4},{5,7},{7,5},{8,10},{10,8},{9,1... | collective-permute-start | bytes 393224 | tf_op jit(solution)/shard_map/ppermute | solution.py:38
  13.6 0.0 collective-permute-done.2
  13.6 2.9 %collective-permute-done.1 = bf16[128,512]{1,0:T(8,128)(2,1)S(1)} collective-permute-done((bf16[128,512]{1,0:T(8,128)(2,1)S(1)}, bf16[128,512]{1,0:T(8,128)(2,1)S(1)}, u32[]{:S(2)}, u32[]{:S(2)}) %collective-permute-start.1) | collective-permute-done | bytes 131104 | tf_op jit(solution)/shard_map/ppermute | solution.py:38
  16.5 2.4 %collective-permute-start.5 = (bf16[128,512]{1,0:T(8,128)(2,1)S(1)}, bf16[128,512]{1,0:T(8,128)(2,1)S(1)}, u32[]{:S(2)}, u32[]{:S(2)}) collective-permute-start(bf16[128,512]{1,0:T(8,128)(2,1)S(1)} %collective-permute-done.1), channel_id=1, source_target_pairs={{0,2},{2,0},{1,3},{3,1},{4,6},{6,4},{5,7},{7,5},{8,10},{10,8},{9,1... | collective-permute-start | bytes 393224 | tf_op jit(solution)/shard_map/ppermute | solution.py:38
  18.9 0.1 pad_maximum_fusion.refs_4_
  19.0 0.1 collective-permute-start.7
  19.1 0.0 collective-permute-done.6
  19.1 0.0 collective-permute-done.4
  19.1 2.8 %collective-permute-done.5 = bf16[128,512]{1,0:T(8,128)(2,1)S(1)} collective-permute-done((bf16[128,512]{1,0:T(8,128)(2,1)S(1)}, bf16[128,512]{1,0:T(8,128)(2,1)S(1)}, u32[]{:S(2)}, u32[]{:S(2)}) %collective-permute-start.5) | collective-permute-done | bytes 131104 | tf_op jit(solution)/shard_map/ppermute | solution.py:38
  21.8 0.1 pad_maximum_fusion.1.refs_5_
  21.9 0.1 collective-permute-start.8
  22.0 0.0 collective-permute-done.7.refs_6_
  22.0 1.9 %collective-permute-done.8.refs_7_ = bf16[4,128,512]{2,1,0:T(8,128)(2,1)S(1)} collective-permute-done((bf16[4,128,512]{2,1,0:T(8,128)(2,1)S(1)}, bf16[4,128,512]{2,1,0:T(8,128)(2,1)S(1)}, u32[]{:S(2)}, u32[]{:S(2)}) %collective-permute-start.8) | collective-permute-done | bytes 524320 | tf_op jit(solution)/shard_map/ppermute | solution.py:38
  23.9 12.6 %shard_map.56 = bf16[1,64,64,512]{3,2,1,0:T(8,128)(2,1)} custom-call(s32[2,8]{1,0:T(2,128)} %bitcast.18, bf16[2,320,160]{2,1,0:T(8,128)(2,1)S(1)} %get-tuple-element.17.refs_1_, bf16[2,512,256]{2,1,0:T(8,128)(2,1)S(1)} %get-tuple-element.18.refs_2_, f32[64,128]{1,0:T(8,128)S(1)} %get-tuple-element.19.refs_3_, ...), custom_call_target="tpu_custom_call" | custom-call | tf_op jit(solution)/shard_map/pallas_call | solution.py:293
  (2 shorter events, 0.0 us)
Async XLA Ops:
  0.0 1.0 %copy-start = (bf16[256,512]{1,0:T(8,128)(2,1)S(1)}, bf16[256,512]{1,0:T(8,128)(2,1)}, u32[]{:S(2)}) copy-start(bf16[256,512]{1,0:T(8,128)(2,1)} %param.5) | copy-start | bytes 786436
  1.0 8.8 %collective-permute-start = (bf16[128,512]{1,0:T(8,128)(2,1)S(1)}, bf16[128,512]{1,0:T(8,128)(2,1)S(1)}, u32[]{:S(2)}, u32[]{:S(2)}) collective-permute-start(bf16[128,512]{1,0:T(8,128)(2,1)S(1)} %constant_dynamic-slice_fusion), channel_id=1, source_target_pairs={{0,4},{4,8},{8,12},{12,0},{1,5},{5,9},{9,13},{13,1},{2,6},{6,10},{... | collective-permute-start | bytes 393224 | tf_op jit(solution)/shard_map/ppermute | solution.py:38
  4.0 9.5 %collective-permute-start.2 = (bf16[128,512]{1,0:T(8,128)(2,1)S(1)}, bf16[128,512]{1,0:T(8,128)(2,1)S(1)}, u32[]{:S(2)}, u32[]{:S(2)}) collective-permute-start(bf16[128,512]{1,0:T(8,128)(2,1)S(1)} %constant_dynamic-slice_fusion), channel_id=1, source_target_pairs={{0,2},{2,0},{1,3},{3,1},{4,6},{6,4},{5,7},{7,5},{8,10},{10,8},{9,1... | collective-permute-start | bytes 393224 | tf_op jit(solution)/shard_map/ppermute | solution.py:38
  5.5 6.8 %collective-permute-start.3 = (bf16[128,512]{1,0:T(8,128)(2,1)S(1)}, bf16[128,512]{1,0:T(8,128)(2,1)S(1)}, u32[]{:S(2)}, u32[]{:S(2)}) collective-permute-start(bf16[128,512]{1,0:T(8,128)(2,1)S(1)} %constant_dynamic-slice_fusion), channel_id=1, source_target_pairs={{0,12},{4,0},{8,4},{12,8},{1,13},{5,1},{9,5},{13,9},{2,14},{6,2},{... | collective-permute-start | bytes 393224 | tf_op jit(solution)/shard_map/ppermute | solution.py:38
  9.7 6.8 %collective-permute-start.1 = (bf16[128,512]{1,0:T(8,128)(2,1)S(1)}, bf16[128,512]{1,0:T(8,128)(2,1)S(1)}, u32[]{:S(2)}, u32[]{:S(2)}) collective-permute-start(bf16[128,512]{1,0:T(8,128)(2,1)S(1)} %collective-permute-done), channel_id=1, source_target_pairs={{0,4},{4,8},{8,12},{12,0},{1,5},{5,9},{9,13},{13,1},{2,6},{6,10},{... | collective-permute-start | bytes 393224 | tf_op jit(solution)/shard_map/ppermute | solution.py:38
  9.7 9.4 %collective-permute-start.4 = (bf16[128,512]{1,0:T(8,128)(2,1)S(1)}, bf16[128,512]{1,0:T(8,128)(2,1)S(1)}, u32[]{:S(2)}, u32[]{:S(2)}) collective-permute-start(bf16[128,512]{1,0:T(8,128)(2,1)S(1)} %collective-permute-done), channel_id=1, source_target_pairs={{0,2},{2,0},{1,3},{3,1},{4,6},{6,4},{5,7},{7,5},{8,10},{10,8},{9,1... | collective-permute-start | bytes 393224 | tf_op jit(solution)/shard_map/ppermute | solution.py:38
  12.4 6.7 %collective-permute-start.6 = (bf16[128,512]{1,0:T(8,128)(2,1)S(1)}, bf16[128,512]{1,0:T(8,128)(2,1)S(1)}, u32[]{:S(2)}, u32[]{:S(2)}) collective-permute-start(bf16[128,512]{1,0:T(8,128)(2,1)S(1)} %collective-permute-done.3), channel_id=1, source_target_pairs={{0,2},{2,0},{1,3},{3,1},{4,6},{6,4},{5,7},{7,5},{8,10},{10,8},{9,1... | collective-permute-start | bytes 393224 | tf_op jit(solution)/shard_map/ppermute | solution.py:38
  16.5 5.4 %collective-permute-start.5 = (bf16[128,512]{1,0:T(8,128)(2,1)S(1)}, bf16[128,512]{1,0:T(8,128)(2,1)S(1)}, u32[]{:S(2)}, u32[]{:S(2)}) collective-permute-start(bf16[128,512]{1,0:T(8,128)(2,1)S(1)} %collective-permute-done.1), channel_id=1, source_target_pairs={{0,2},{2,0},{1,3},{3,1},{4,6},{6,4},{5,7},{7,5},{8,10},{10,8},{9,1... | collective-permute-start | bytes 393224 | tf_op jit(solution)/shard_map/ppermute | solution.py:38
  19.0 3.0 %collective-permute-start.7 = (bf16[4,128,512]{2,1,0:T(8,128)(2,1)S(1)}, bf16[4,128,512]{2,1,0:T(8,128)(2,1)S(1)}, u32[]{:S(2)}, u32[]{:S(2)}) collective-permute-start(bf16[4,128,512]{2,1,0:T(8,128)(2,1)S(1)} %pad_maximum_fusion.refs_4_), channel_id=1, source_target_pairs={{0,1},{1,0},{2,3},{3,2},{4,5},{5,4},{6,7},{7,6},{8,9},{9,8},{10,11... | collective-permute-start | bytes 1572872 | tf_op jit(solution)/shard_map/ppermute | solution.py:38
  21.9 2.0 %collective-permute-start.8 = (bf16[4,128,512]{2,1,0:T(8,128)(2,1)S(1)}, bf16[4,128,512]{2,1,0:T(8,128)(2,1)S(1)}, u32[]{:S(2)}, u32[]{:S(2)}) collective-permute-start(bf16[4,128,512]{2,1,0:T(8,128)(2,1)S(1)} %pad_maximum_fusion.1.refs_5_), channel_id=1, source_target_pairs={{0,1},{1,0},{2,3},{3,2},{4,5},{5,4},{6,7},{7,6},{8,9},{9,8},{10,11... | collective-permute-start | bytes 1572872 | tf_op jit(solution)/shard_map/ppermute | solution.py:38
